TPU v7x, 32 devices: a whole 2x2x4 slice. The times are simulated.
32 devices in a mesh: ctx: 8 (over z, y), wa: 4 (over x, core).
Axes of the slice: x: 2, y: 2, z: 4, core: 2. Of those that a mesh axis runs over, the one named last changes fastest.
Arguments:
- tokens: bfloat16 [4, 1024, 896], P('wa', 'ctx'), may hold values from -6 to 6
- neighbours: bfloat16 [4, 16, 256, 896], P('wa', 'ctx'), may hold values from -6 to 6
- teacher: bfloat16 [4, 1024, 896], P('wa', 'ctx'), may hold values from -6 to 6
- valid_mask: int32 [4, 1024], P('wa', 'ctx'), may hold values from 0 to 1, as said below
- block_order: int32 [16], replicated, may hold values from 0 to 15, as said below
- query_weight: bfloat16 [896, 1024], P('wa'), may hold values from -0.1875 to 0.1875
- key_weight: bfloat16 [896, 1024], P('wa'), may hold values from -0.1875 to 0.1875
- value_weight: bfloat16 [896, 1024], P('wa'), may hold values from -0.1875 to 0.1875
- output_weight: bfloat16 [1024, 896], P('wa'), may hold values from -3 to 3
- relative_weight: bfloat16 [896, 1024], P('wa'), may hold values from -0.1875 to 0.1875
- content_bias: bfloat16 [1024], P('wa'), may hold values from -3 to 3
- position_bias: bfloat16 [1024], P('wa'), may hold values from -3 to 3
- cross_query_weight: bfloat16 [896, 1024], P('wa'), may hold values from -0.1875 to 0.1875
- cross_key_weight: bfloat16 [896, 1024], P('wa'), may hold values from -0.1875 to 0.1875
- cross_value_weight: bfloat16 [896, 1024], P('wa'), may hold values from -0.1875 to 0.1875
- cross_output_weight: bfloat16 [1024, 896], P('wa'), may hold values from -1.5 to 1.5
- up_weight: bfloat16 [896, 3584], P('wa'), may hold values from -0.1875 to 0.1875
- down_weight: bfloat16 [3584, 896], P('wa'), may hold values from -0.09375 to 0.09375
- attention_gain: bfloat16 [896], P('wa'), may hold values from 0.5 to 1.5
- cross_gain: bfloat16 [896], P('wa'), may hold values from 0.5 to 1.5
- feedforward_gain: bfloat16 [896], P('wa'), may hold values from 0.5 to 1.5
Outputs:
- layer_out: float32 [4, 1024, 896], P('wa', 'ctx')
- loss: float32 [], replicated
- tokens_grad: float32 [4, 1024, 896], P('wa', 'ctx')
- neighbours_grad: float32 [4, 16, 256, 896], P('wa', 'ctx')
- query_weight_grad: float32 [896, 1024], P('wa')
- key_weight_grad: float32 [896, 1024], P('wa')
- value_weight_grad: float32 [896, 1024], P('wa')
- output_weight_grad: float32 [1024, 896], P('wa')
- relative_weight_grad: float32 [896, 1024], P('wa')
- content_bias_grad: float32 [1024], P('wa')
- position_bias_grad: float32 [1024], P('wa')
- cross_query_weight_grad: float32 [896, 1024], P('wa')
- cross_key_weight_grad: float32 [896, 1024], P('wa')
- cross_value_weight_grad: float32 [896, 1024], P('wa')
- cross_output_weight_grad: float32 [1024, 896], P('wa')
- up_weight_grad: float32 [896, 3584], P('wa')
- down_weight_grad: float32 [3584, 896], P('wa')
- attention_gain_grad: float32 [896], P('wa')
- cross_gain_grad: float32 [896], P('wa')
- feedforward_gain_grad: float32 [896], P('wa')
Inputs may be any that keep to these rules, and one draw needn't show every extreme that they name: `block_order`: a permutation of 0 to 15 in which entries 2 k and 2 k + 1 are p and 15 - p for some p. `valid_mask`: each entry 0 or 1; the entry of every stored position t with t % 16 == 15 is 1.
All inputs are finite; a program needn't handle non-finite values.
Results may differ from a plain program's by a relative error of at most 0.029.
Values may be sent and summed in bfloat16 or wider, within the bound.
A program may use at most 512 MiB of HBM per device.

v0:
```python
import functools
import types

import jax
import jax.numpy as jnp
from jax import lax
from jax.experimental import pallas as pl
from jax.experimental.pallas import tpu as pltpu
from jax.sharding import PartitionSpec as P

HEADS = 16
HEAD_DIM = 64
GROUP = 64
NK = 256
TILE = 128

eps_norm = 1e-06
neg_big = -1e30
highest = lax.Precision.HIGHEST
f32 = jnp.float32
bf16 = jnp.bfloat16


def inverse_rms(hidden):
    return lax.rsqrt(jnp.mean(hidden * hidden, axis=-1, keepdims=True) + eps_norm)


def norm_pull(hidden, scale, gain, grad):
    scaled = grad * gain
    mean = jnp.mean(hidden * scaled, axis=-1, keepdims=True)
    return scale * scaled - hidden * (scale * scale * scale) * mean


def gelu_tanh(value):
    return jax.nn.gelu(value, approximate=True)


def sinusoid(distance, width):
    half = width // 2
    freq = jnp.exp(-jnp.log(10000.0) * jnp.arange(half, dtype=f32) * 2.0 / width)
    angle = distance[:, None] * freq[None, :]
    return jnp.concatenate([jnp.sin(angle), jnp.cos(angle)], axis=1)


def dot_nn(a, b):
    return lax.dot_general(a, b, (((1,), (0,)), ((), ())), preferred_element_type=f32)


def dot_nt(a, b):
    return lax.dot_general(a, b, (((1,), (1,)), ((), ())), preferred_element_type=f32)


def dot_tn(a, b):
    return lax.dot_general(a, b, (((0,), (0,)), ((), ())), preferred_element_type=f32)


def swap(value, axis, bit):
    pairs = [(i, i ^ bit) for i in range(lax.axis_size(axis))]
    return lax.ppermute(value, axis, pairs)


def bits_of(axis):
    bits, bit = [], 1
    while bit < lax.axis_size(axis):
        bits.append(bit)
        bit *= 2
    return bits


def my_bit(axis, bit):
    return (lax.axis_index(axis) // bit) % 2


def ordered(bit, own, other, dim):
    return jnp.where(
        bit == 0,
        jnp.concatenate([own, other], axis=dim),
        jnp.concatenate([other, own], axis=dim),
    )


def split(value, bit, dim):
    half = value.shape[dim] // 2
    keep = lax.dynamic_slice_in_dim(value, bit * half, half, dim)
    send = lax.dynamic_slice_in_dim(value, (1 - bit) * half, half, dim)
    return keep, send


def gather_parts(value):
    parts = {0: value}
    for bit in reversed(bits_of("wa")):
        parts.update({r | bit: swap(part, "wa", bit) for r, part in list(parts.items())})
    return [parts[r] for r in sorted(parts)]


def scatter_parts(parts):
    parts = dict(enumerate(parts))
    for bit in bits_of("wa"):
        kept = {}
        for r, part in parts.items():
            if not r & bit:
                got = swap(parts[r | bit].astype(bf16), "wa", bit)
                kept[r] = part + got.astype(f32)
        parts = kept
    return parts[0]


def take_columns(weight):
    value = weight[None]
    for bit in reversed(bits_of("wa")):
        mine = my_bit("wa", bit)
        keep, send = split(value, mine, 2)
        value = ordered(mine, keep[:, None], swap(send, "wa", bit)[:, None], 1)
        value = value.reshape((-1,) + value.shape[2:])
    return value.reshape(-1, value.shape[-1])


def spread_columns(value):
    for bit in bits_of("wa"):
        mine = my_bit("wa", bit)
        paired = value.reshape((value.shape[0], value.shape[1] // 2, 2) + value.shape[2:])
        keep, send = split(paired, mine, 2)
        value = ordered(mine, keep[:, :, 0], swap(send[:, :, 0], "wa", bit), 3)
    return value[:, 0]


def halving_dim(shape):
    if shape[-2] % 16 == 0:
        return len(shape) - 2
    if shape[0] % 2 == 0:
        return 0
    if shape[-2] % 2 == 0:
        return len(shape) - 2
    return len(shape) - 1


def sum_over_ctx(value, bits, finish):
    dims = []
    for bit in bits:
        dim = halving_dim(value.shape)
        keep, send = split(value, my_bit("ctx", bit), dim)
        value = (keep.astype(f32) + swap(send, "ctx", bit).astype(f32)).astype(bf16)
        dims.append(dim - value.ndim if dim else 0)
    value = finish(value)
    for bit, dim in reversed(list(zip(bits, dims))):
        dim = dim % value.ndim
        value = ordered(my_bit("ctx", bit), value, swap(value, "ctx", bit), dim)
    return value


def all_summed(value, axis):
    for bit in bits_of(axis):
        value = value + swap(value, axis, bit)
    return value


def sum_column_grads(grads):
    places = lax.axis_size("wa")
    grads = grads.reshape(grads.shape[0], places, grads.shape[1] // places, grads.shape[2])
    bits = bits_of("ctx")
    if grads.shape[2] % lax.axis_size("ctx") == 0:
        return sum_over_ctx(grads, bits, spread_columns).astype(f32)
    return sum_over_ctx(spread_columns(grads), bits, lambda value: value).astype(f32)


def sum_row_grads(grads):
    return sum_over_ctx(grads[None], bits_of("ctx"), lambda value: value)[0].astype(f32)


def first_half(shape):
    return lax.broadcasted_iota(jnp.int32, shape, 1) < HEAD_DIM


def stack_heads(rows):
    mask = first_half(rows.shape)
    zero = jnp.zeros_like(rows)
    return jnp.concatenate([jnp.where(mask, rows, zero), jnp.where(mask, zero, rows)], axis=0)


def join_heads(stacked):
    rows = stacked.shape[0] // 2
    return jnp.where(first_half((rows, stacked.shape[1])), stacked[:rows], stacked[rows:])


def copy_blocks(order_ref, source, target, block, inward):
    for place in range(source.shape[0] // block):
        start = pl.multiple_of(order_ref[place] * block, block)
        if inward:
            target[place * block : (place + 1) * block, :] = source[pl.ds(start, block), :]
        else:
            target[pl.ds(start, block), :] = source[place * block : (place + 1) * block, :]


def attention_shares(content, position, key_ref, rel_ref, row_start, seq_len):
    length = row_start + TILE
    wide_len = length + TILE
    offset = seq_len - TILE - row_start
    scale = HEAD_DIM ** (-0.5)
    scores = dot_nt(content, key_ref[0:length, :])
    wide = dot_nt(position, rel_ref[offset : offset + wide_len, :])
    halves = []
    for head in range(2):
        part = wide[head * TILE : (head + 1) * TILE]
        turned = pltpu.roll(part, wide_len - (TILE - 1), 1, stride=1, stride_axis=0)
        halves.append(turned[:, :length])
    scores = (scores + jnp.concatenate(halves, axis=0)) * scale
    row = lax.broadcasted_iota(jnp.int32, scores.shape, 0) % TILE + row_start
    col = lax.broadcasted_iota(jnp.int32, scores.shape, 1)
    scores = jnp.where(col <= row, scores, neg_big)
    top = jnp.max(scores, axis=1, keepdims=True)
    raised = jnp.exp(scores - top)
    total = jnp.sum(raised, axis=1, keepdims=True)
    return raised * (1.0 / total)


def attend_tiles(qkv, rel_ref, content_bias, position_bias, out):
    seq_len = qkv.shape[0]
    keys = qkv.at[:, 128:256]
    values = qkv.at[:, 256:384]
    for tile in range(seq_len // TILE):
        start = tile * TILE
        query = qkv[start : start + TILE, 0:128].astype(f32)
        content = stack_heads((query + content_bias).astype(bf16))
        position = stack_heads((query + position_bias).astype(bf16))
        shares = attention_shares(content, position, keys, rel_ref, start, seq_len)
        got = dot_nn(shares.astype(bf16), values[0 : start + TILE, :])
        got = join_heads(got).astype(bf16)
        block = out.shape[1]
        for part in range(TILE // block):
            out[start // block + part] = got[part * block : (part + 1) * block]


def attend_back_tiles(
    qkv, grad, rel_ref, content_bias, position_bias, dqkv, dkey, dvalue, drel, poll
):
    scale = HEAD_DIM ** (-0.5)
    seq_len = qkv.shape[0]
    block = dqkv.shape[1]
    keys = qkv.at[:, 128:256]
    values = qkv.at[:, 256:384]
    dkey[...] = jnp.zeros_like(dkey)
    dvalue[...] = jnp.zeros_like(dvalue)
    drel[...] = jnp.zeros_like(drel)
    row = lax.broadcasted_iota(jnp.int32, (TILE, TILE), 0)
    col = lax.broadcasted_iota(jnp.int32, (TILE, TILE), 1)
    flip = jnp.where(row + col == TILE - 1, 1.0, 0.0).astype(bf16)
    content_sum = jnp.zeros((1, 128), f32)
    position_sum = jnp.zeros((1, 128), f32)
    for tile in range(seq_len // TILE):
        poll(tile)
        start = tile * TILE
        length = start + TILE
        wide_len = length + TILE
        offset = seq_len - TILE - start
        query = qkv[start : start + TILE, 0:128].astype(f32)
        content = stack_heads((query + content_bias).astype(bf16))
        plain = (query + position_bias).astype(bf16)
        position = stack_heads(plain)
        shares = attention_shares(content, position, keys, rel_ref, start, seq_len)
        out_grad = stack_heads(grad[start : start + TILE, :])
        share_grad = dot_nt(out_grad, values[0:length, :])
        delta = jnp.sum(shares * share_grad, axis=1, keepdims=True)
        score_grad = (shares * (share_grad - delta)).astype(bf16)
        content_grad = join_heads(dot_nn(score_grad, keys[0:length, :])) * scale
        parts = []
        for head in range(2):
            turned = dot_nn(flip, score_grad[head * TILE : (head + 1) * TILE])
            turned = jnp.concatenate([turned, jnp.zeros((TILE, TILE), f32)], axis=1)
            parts.append(pltpu.roll(turned, 0, 1, stride=1, stride_axis=0))
        wide_grad = jnp.concatenate(parts, axis=0).astype(bf16)
        relative = rel_ref[offset : offset + wide_len, :]
        turned_grad = join_heads(dot_nn(wide_grad, relative)) * scale
        turned_rows = stack_heads(dot_nn(flip, plain).astype(bf16))
        drel[offset : offset + wide_len, :] += dot_tn(wide_grad, turned_rows)
        high = turned_grad.astype(bf16)
        low = (turned_grad - high.astype(f32)).astype(bf16)
        position_grad = dot_nn(flip, high) + dot_nn(flip, low)
        content_sum += jnp.sum(content_grad, axis=0, keepdims=True)
        position_sum += jnp.sum(turned_grad, axis=0, keepdims=True)
        query_grad = (content_grad + position_grad).astype(bf16)
        for part in range(TILE // block):
            dqkv[start // block + part, :, 0:128] = query_grad[part * block : (part + 1) * block]
        dkey[0:length, :] += dot_tn(score_grad, content)
        dvalue[0:length, :] += dot_tn(shares.astype(bf16), out_grad)
    for part in range(seq_len // block):
        rows = slice(part * block, (part + 1) * block)
        dqkv[part, :, 128:256] = (dkey[rows, :] * scale).astype(bf16)
        dqkv[part, :, 256:384] = dvalue[rows, :].astype(bf16)
    return content_sum, position_sum


in_vmem = pl.BlockSpec(memory_space=pltpu.VMEM)
in_smem = pl.BlockSpec(memory_space=pltpu.SMEM)


def head_mask(shape, head):
    lane = lax.broadcasted_iota(jnp.int32, shape, 1)
    return (lane >= head * HEAD_DIM) & (lane < (head + 1) * HEAD_DIM)


def stack_all(rows):
    zero = jnp.zeros_like(rows)
    heads = rows.shape[1] // HEAD_DIM
    return jnp.concatenate(
        [jnp.where(head_mask(rows.shape, head), rows, zero) for head in range(heads)], axis=0
    )


def join_all(stacked):
    heads = stacked.shape[1] // HEAD_DIM
    rows = stacked.shape[0] // heads
    out = jnp.zeros((rows, stacked.shape[1]), stacked.dtype)
    for head in range(heads):
        part = stacked[head * rows : (head + 1) * rows]
        out = jnp.where(head_mask(part.shape, head), part, out)
    return out


def cross_shares(query, keys):
    scores = dot_nt(query, keys) * (HEAD_DIM ** (-0.5))
    raised = jnp.exp(scores - jnp.max(scores, axis=1, keepdims=True))
    return raised / jnp.sum(raised, axis=1, keepdims=True)


def cross_forward_kernel(q_ref, kv_ref, out_ref):
    width = q_ref.shape[1]
    shares = cross_shares(stack_all(q_ref[...]), kv_ref[:, 0:width])
    out_ref[...] = join_all(dot_nn(shares.astype(bf16), kv_ref[:, width:])).astype(bf16)


def cross_backward_kernel(q_ref, kv_ref, grad_ref, dq_ref, dkv_ref):
    width = q_ref.shape[1]
    scale = HEAD_DIM ** (-0.5)
    keys = kv_ref[:, 0:width]
    query = stack_all(q_ref[...])
    grad = stack_all(grad_ref[...])
    shares = cross_shares(query, keys)
    share_grad = dot_nt(grad, kv_ref[:, width:])
    delta = jnp.sum(shares * share_grad, axis=1, keepdims=True)
    score_grad = (shares * (share_grad - delta)).astype(bf16)
    dq_ref[...] = (join_all(dot_nn(score_grad, keys)) * scale).astype(bf16)
    dkv_ref[:, 0:width] = (dot_tn(score_grad, query) * scale).astype(bf16)
    dkv_ref[:, width:] = dot_tn(shares.astype(bf16), grad).astype(bf16)


def cross_forward(query, pair):
    width = query.shape[1]
    groups = query.shape[0] // GROUP
    return pl.pallas_call(
        cross_forward_kernel,
        out_shape=jax.ShapeDtypeStruct(query.shape, bf16),
        grid=(groups,),
        in_specs=[
            pl.BlockSpec((GROUP, width), lambda g: (g, 0)),
            pl.BlockSpec((NK, 2 * width), lambda g: (g, 0)),
        ],
        out_specs=pl.BlockSpec((GROUP, width), lambda g: (g, 0)),
        cost_estimate=pl.CostEstimate(
            flops=groups * 4 * 256 * 256 * 256, bytes_accessed=groups * 330000, transcendentals=groups * 65536
        ),
        name="cross_forward",
    )(query, pair)


def cross_backward(query, pair, grad):
    width = query.shape[1]
    groups = query.shape[0] // GROUP
    return pl.pallas_call(
        cross_backward_kernel,
        out_shape=[
            jax.ShapeDtypeStruct(query.shape, bf16),
            jax.ShapeDtypeStruct(pair.shape, bf16),
        ],
        grid=(groups,),
        in_specs=[
            pl.BlockSpec((GROUP, width), lambda g: (g, 0)),
            pl.BlockSpec((NK, 2 * width), lambda g: (g, 0)),
            pl.BlockSpec((GROUP, width), lambda g: (g, 0)),
        ],
        out_specs=[
            pl.BlockSpec((GROUP, width), lambda g: (g, 0)),
            pl.BlockSpec((NK, 2 * width), lambda g: (g, 0)),
        ],
        cost_estimate=pl.CostEstimate(
            flops=groups * 10 * 256 * 256 * 256, bytes_accessed=groups * 660000, transcendentals=groups * 65536
        ),
        name="cross_backward",
    )(query, pair, grad)


mesh_id = pl.DeviceIdType.MESH


def signal_to(barrier, ctx, wa):
    pl.semaphore_signal(barrier, inc=1, device_id=(ctx, wa), device_id_type=mesh_id)


def tree_sum(values):
    while len(values) > 1:
        values = [a + b for a, b in zip(values[::2], values[1::2])]
    return values[0]


def gelu_slope(value):
    inner = 0.7978845608028654 * (value + 0.044715 * value * value * value)
    turned = jnp.tanh(inner)
    slope = 0.7978845608028654 * (1.0 + 3.0 * 0.044715 * value * value)
    return 0.5 * (1.0 + turned) + 0.5 * value * (1.0 - turned * turned) * slope


def places_here():
    return lax.axis_index("ctx"), lax.axis_index("wa")


def meet_all():
    c, w = places_here()
    owner = c // 2
    own = owner == w
    barrier = pltpu.get_barrier_semaphore()
    for j in range(1, 8):
        signal_to(barrier, c ^ j, w)
    for j in range(1, 4):
        signal_to(barrier, c, w ^ j)
    for j in range(1, 8):
        signal_to(barrier, c ^ j, owner)
    for r in range(4):
        for h in range(2):

            @pl.when(jnp.logical_not(jnp.logical_and(2 * w + h == c, r == 0)))
            def _(r=r, h=h):
                signal_to(barrier, 2 * w + h, w ^ r)

    @pl.when(jnp.logical_not(own))
    def _():
        signal_to(barrier, c, owner)

    pl.semaphore_wait(barrier, 26 - 2 * own.astype(jnp.int32))


def meet_lines():
    c, w = places_here()
    barrier = pltpu.get_barrier_semaphore()
    for j in range(1, 8):
        signal_to(barrier, c ^ j, w)
    for j in range(1, 4):
        signal_to(barrier, c, w ^ j)
    pl.semaphore_wait(barrier, 10)


def remote(source, target, send, recv, ctx, wa):
    return pltpu.make_async_remote_copy(
        src_ref=source,
        dst_ref=target,
        send_sem=send,
        recv_sem=recv,
        device_id=(ctx, wa),
        device_id_type=mesh_id,
    )


class GatherRows:

    def __init__(self, buf, send, recv):
        self.buf, self.send, self.recv = buf, send, recv
        self.c, self.w = places_here()

    def copy(self, k):
        source, entry, j = ((0, 1, 1), (0, 2, 2), (2, 3, 1))[k]
        return remote(
            self.buf.at[source],
            self.buf.at[entry],
            self.send.at[k],
            self.recv.at[k],
            self.c,
            self.w ^ j,
        )

    def start(self):
        self.copy(1).start()
        self.copy(0).start()

    def near(self):
        self.copy(0).wait()

    def relay(self):
        self.copy(1).wait()
        self.copy(2).start()

    def far(self):
        self.copy(2).wait()


class SumRows:

    def __init__(self, out_buf, in_buf, send, recv):
        self.out, self.inn, self.send, self.recv = out_buf, in_buf, send, recv
        self.c, self.w = places_here()

    def copy(self, k):
        j = (1, 1, 2)[k]
        return remote(
            self.out.at[k], self.inn.at[k], self.send.at[k], self.recv.at[k], self.c, self.w ^ j
        )

    def give_near(self, value):
        self.out[0] = value.astype(bf16)
        self.copy(0).start()

    def give_far(self, value):
        self.out[1] = value.astype(bf16)
        self.copy(1).start()

    def pass_on(self, value):
        self.copy(1).wait()
        self.out[2] = (value + self.inn[1].astype(f32)).astype(bf16)
        self.copy(2).start()

    def total(self, value):
        self.copy(0).wait()
        value = value + self.inn[0].astype(f32)
        self.copy(2).wait()
        return value + self.inn[2].astype(f32)


class CtxSum:

    def __init__(self, send, recv, x=None, half=None, part=None, share=None, out=None, spread=0):
        self.send, self.recv = send, recv
        self.x, self.half, self.part, self.share, self.out = x, half, part, share, out
        self.spread = spread
        self.c, self.w = places_here()
        self.z, self.y = self.c // 2, self.c % 2

    def y_copy(self):
        return remote(
            self.x.at[:, 1 - self.y], self.half, self.send.at[0], self.recv.at[0], self.c ^ 1, self.w
        )

    def start_y(self):
        self.y_copy().start()

    def finish_y(self):
        self.y_copy().wait()
        for z in range(4):
            mine = self.x[z, self.y].astype(f32)
            self.half[z] = (self.half[z].astype(f32) + mine).astype(bf16)

    def z_copy(self, j):
        return remote(
            self.half.at[self.z ^ j],
            self.part.at[j - 1],
            self.send.at[j],
            self.recv.at[j],
            self.c ^ (2 * j),
            self.w,
        )

    def start_z(self):
        for j in (2, 3, 1):
            self.z_copy(j).start()

    def finish_z(self):
        total = self.half[self.z].astype(f32)
        for j in (1, 2, 3):
            self.z_copy(j).wait()
            total = total + self.part[j - 1].astype(f32)
        self.share[...] = total.astype(bf16)

    def columns(self, place):
        width = self.spread
        return self.out.at[self.z, self.y, :, pl.ds(pl.multiple_of(place * width, 128), width)]

    def wa_copy(self, j, place):
        return remote(
            self.share.at[self.w ^ j],
            self.columns(place),
            self.send.at[3 + j],
            self.recv.at[3 + j],
            self.c,
            self.w ^ j,
        )

    def own_copy(self):
        source = self.share.at[self.w] if self.spread else self.share
        target = self.columns(self.w) if self.spread else self.out.at[self.z, self.y]
        return pltpu.make_async_copy(source, target, self.send.at[11])

    def start_wa(self):
        if self.spread:
            for j in (2, 3, 1):
                self.wa_copy(j, self.w).start()
        self.own_copy().start()

    def finish_wa(self):
        self.own_copy().wait()
        if self.spread:
            for j in (1, 2, 3):
                self.wa_copy(j, self.w).wait_send()
                self.wa_copy(j, self.w ^ j).wait_recv()

    def back_z_copy(self, j, z):
        mine = self.out.at[z, self.y]
        return remote(mine, mine, self.send.at[6 + j], self.recv.at[6 + j], self.c ^ (2 * j), self.w)

    def start_back_z(self):
        for j in (2, 3, 1):
            self.back_z_copy(j, self.z).start()

    def finish_back_z(self):
        for j in (1, 2, 3):
            self.back_z_copy(j, self.z).wait_send()
            self.back_z_copy(j, self.z ^ j).wait_recv()

    def back_y_copy(self, y):
        part = self.out.at[:, y]
        return remote(part, part, self.send.at[10], self.recv.at[10], self.c ^ 1, self.w)

    def start_back_y(self):
        self.back_y_copy(self.y).start()

    def finish_back_y(self):
        self.back_y_copy(self.y).wait_send()
        self.back_y_copy(1 - self.y).wait_recv()


def put_shares(target, grads, first=0):
    count = grads.shape[0] // 32
    padded = target.shape[3]
    for place in range(4):
        for share in range(8):
            start = (place * 8 + share) * count
            part = grads[start : start + count]
            part = jnp.concatenate([part, jnp.zeros((padded - count, part.shape[1]), f32)], axis=0)
            target[share // 2, share % 2, place, :, first : first + part.shape[1]] = part.astype(bf16)


def put_rows(target, grads):
    count = grads.shape[0] // 8
    for share in range(8):
        target[share // 2, share % 2] = grads[share * count : (share + 1) * count].astype(bf16)


class Cut:

    def __init__(self, ref, start):
        self.ref, self.start = ref, start

    @property
    def at(self):
        return self

    def __getitem__(self, k):
        return self.ref.at[self.start + k]


class Pool:
    def __init__(self, ref):
        self.ref, self.used = ref, 0

    def take(self, count):
        cut = Cut(self.ref, self.used)
        self.used += count
        return cut


class LineGather:

    def __init__(self, out, send, recv):
        self.out, self.send, self.recv = out, send, recv
        self.c, self.w = places_here()
        self.z = self.c // 2
        self.right, self.left = self.z < 3, self.z > 0

    def y_copy(self, block, slot):
        ref = self.out.at[block]
        return remote(ref, ref, self.send.at[slot], self.recv.at[slot], self.c ^ 1, self.w)

    def z_copy(self, block, slot, step):
        k = slot + (7 if step > 0 else 10)
        ref = self.out.at[block]
        return remote(ref, ref, self.send.at[k], self.recv.at[k], self.c + step, self.w)

    def start(self):
        @pl.when(self.right)
        def _():
            self.z_copy(self.c, 0, 2).start()

        @pl.when(self.left)
        def _():
            self.z_copy(self.c, 0, -2).start()

        self.y_copy(self.c, 0).start()

    def step(self, t):
        @pl.when(self.z > t)
        def _():
            block = self.c - 2 * (t + 1)
            self.z_copy(block, t, 2).wait_recv()
            if t < 2:

                @pl.when(self.right)
                def _():
                    self.z_copy(block, t + 1, 2).start()

            self.y_copy(block, t + 1).start()

        @pl.when(self.z < 3 - t)
        def _():
            block = self.c + 2 * (t + 1)
            self.z_copy(block, t, -2).wait_recv()
            if t < 2:

                @pl.when(self.left)
                def _():
                    self.z_copy(block, t + 1, -2).start()

            self.y_copy(block, t + 4).start()

    def finish(self):
        self.y_copy(self.c, 0).wait_send()
        self.y_copy(self.c ^ 1, 0).wait_recv()
        for t in range(3):
            for step, at, near in ((-2, t + 1, self.z > t), (2, t + 4, self.z < 3 - t)):

                @pl.when(near)
                def _(step=step, at=at):
                    self.y_copy(self.c + step * (t + 1), at).wait_send()
                    self.y_copy((self.c ^ 1) + step * (t + 1), at).wait_recv()

        @pl.when(self.right)
        def _():
            self.z_copy(self.c, 0, 2).wait_send()

        @pl.when(self.left)
        def _():
            self.z_copy(self.c, 0, -2).wait_send()

        for t in range(2):

            @pl.when(jnp.logical_and(self.z > t, self.right))
            def _():
                self.z_copy(self.c, t + 1, 2).wait_send()

            @pl.when(jnp.logical_and(self.z < 3 - t, self.left))
            def _():
                self.z_copy(self.c, t + 1, -2).wait_send()


class Columns:

    def __init__(self, source, target, width, first, send, recv, at=None):
        self.source, self.target, self.width, self.first = source, target, width, first
        self.send, self.recv, self.column = send, recv, at
        self.shared = at is None
        self.c, self.w = places_here()
        self.y = self.c % 2

    def taken(self, place, half=None):
        start = place * self.width if self.column is None else self.column
        rows = self.source.shape[0]
        which = slice(None) if half is None else pl.ds(pl.multiple_of(half * (rows // 2), 16), rows // 2)
        return self.source.at[which, pl.ds(pl.multiple_of(start, 128), self.width)]

    def put(self, place, half=None):
        rows = self.source.shape[0]
        start, count = place * rows, rows
        if half is not None:
            start, count = start + half * (rows // 2), rows // 2
        return self.target.at[
            pl.ds(pl.multiple_of(start, 16), count), self.first : self.first + self.width
        ]

    def copy(self, j, place):
        half = self.y if self.shared and j > 1 else None
        return remote(
            self.taken(self.w ^ j, half),
            self.put(place, half),
            self.send.at[j],
            self.recv.at[j],
            self.c,
            self.w ^ j,
        )

    def passed(self, j, half):
        ref = self.put(self.w ^ j, half)
        return remote(ref, ref, self.send.at[2 + j], self.recv.at[2 + j], self.c ^ 1, self.w)

    def own(self):
        return pltpu.make_async_copy(self.taken(self.w), self.put(self.w), self.send.at[0])

    def start(self):
        for j in (2, 3, 1):
            self.copy(j, self.w).start()
        self.own().start()

    def relay(self):
        for j in (2, 3):
            self.copy(j, self.w).wait_send()
            self.copy(j, self.w ^ j).wait_recv()
            self.passed(j, self.y).start()

    def finish(self):
        self.own().wait()
        for j in (1,) if self.shared else (1, 2, 3):
            self.copy(j, self.w).wait_send()
            self.copy(j, self.w ^ j).wait_recv()
        if self.shared:
            for j in (2, 3):
                self.passed(j, self.y).wait_send()
                self.passed(j, 1 - self.y).wait_recv()


class SmallSum:

    def __init__(self, ref, got, axis, send, recv):
        self.ref, self.got, self.axis, self.send, self.recv = ref, got, axis, send, recv
        self.c, self.w = places_here()

    def copy(self, k):
        j = k + 1
        ctx, wa = (self.c ^ j, self.w) if self.axis == "ctx" else (self.c, self.w ^ j)
        return remote(self.ref, self.got.at[k], self.send.at[k], self.recv.at[k], ctx, wa)

    def start(self):
        for k in range(self.got.shape[0]):
            self.copy(k).start()

    def finish(self):
        count = self.got.shape[0]
        for k in range(count):
            self.copy(k).wait()
        self.ref[...] = tree_sum([self.ref[...]] + [self.got[k] for k in range(count)])


class SwapHeads:

    def __init__(self, by_heads, by_rows, outward, send, recv):
        self.heads, self.rows, self.outward = by_heads, by_rows, outward
        self.send, self.recv = send, recv
        self.c, self.w = places_here()
        self.owner, self.half = self.c // 2, self.c % 2
        self.own = self.owner == self.w
        self.other = jnp.logical_not(self.own)

    def lanes(self):
        return pl.ds(pl.multiple_of(self.half * 128, 128), 128)

    def out_copy(self, j):
        slot = self.w ^ self.owner
        return remote(
            self.heads.at[self.c ^ j],
            self.rows.at[slot, :, self.lanes()],
            self.send.at[j],
            self.recv.at[slot * 2 + self.half],
            self.c ^ j,
            self.owner,
        )

    def start_out(self):
        for j in range(7, 0, -1):
            self.out_copy(j).start()

        @pl.when(self.other)
        def _():
            self.out_copy(0).start()

        @pl.when(self.own)
        def _():
            slot = self.w ^ self.owner
            pltpu.make_async_copy(
                self.heads.at[self.c],
                self.rows.at[slot, :, self.lanes()],
                self.recv.at[slot * 2 + self.half],
            ).start()

    def wait_rows(self, r):
        for h in range(2):
            remote(
                self.heads.at[0],
                self.rows.at[r, :, h * 128 : (h + 1) * 128],
                self.send.at[0],
                self.recv.at[r * 2 + h],
                self.c ^ 1,
                self.w,
            ).wait_recv()

    def finish_out(self):
        for j in range(1, 8):
            self.out_copy(j).wait_send()

        @pl.when(self.other)
        def _():
            self.out_copy(0).wait_send()

    def in_copy(self, r, h):
        return remote(
            self.rows.at[r, :, h * 128 : (h + 1) * 128],
            self.heads.at[self.c],
            self.send.at[r * 2 + h],
            self.recv.at[self.c],
            2 * self.w + h,
            self.w ^ r,
        )

    def mine(self, r, h):
        return jnp.logical_and(2 * self.w + h == self.c, r == 0)

    def start_in(self, r):
        for h in range(2):

            @pl.when(jnp.logical_not(self.mine(r, h)))
            def _():
                self.in_copy(r, h).start()

            @pl.when(self.mine(r, h))
            def _():
                pltpu.make_async_copy(
                    self.rows.at[r, :, h * 128 : (h + 1) * 128],
                    self.heads.at[self.c],
                    self.recv.at[self.c],
                ).start()

    def finish_in(self):
        for block in range(8):
            remote(
                self.rows.at[0, :, 0:128],
                self.heads.at[block],
                self.send.at[0],
                self.recv.at[block],
                self.c ^ 1,
                self.w,
            ).wait_recv()
        for r in range(4):
            for h in range(2):

                @pl.when(jnp.logical_not(self.mine(r, h)))
                def _(r=r, h=h):
                    self.in_copy(r, h).wait_send()


def layer_kernel(names, total_tokens, block, *refs):
    v = types.SimpleNamespace(**dict(zip(names, refs, strict=True)))
    c, w = places_here()
    send, recv, local = Pool(v.send), Pool(v.recv), Pool(v.local)
    tok, width = v.tokens.shape
    seq_len = 8 * tok
    rows = 4 * tok
    cols = v.output_w.shape[0]
    hidden = v.down_w.shape[0]
    scale = HEAD_DIM ** (-0.5)

    def load(source, target):
        copy = pltpu.make_async_copy(source, target, local.take(1).at[0])
        copy.start()
        return copy

    near_load = load(v.neighbours, v.near.at[0])
    early = [load(v.waves_any, v.waves)]
    late = [
        load(v.output_any, v.output_w),
        load(v.cross_out_any, v.cross_out_w),
        load(v.down_any, v.down_w),
    ]
    column = lax.broadcasted_iota(jnp.int32, (256, 1024), 1)
    line = lax.broadcasted_iota(jnp.int32, (256, 1024), 0)

    def placed(value, start):
        chosen = jnp.where(column == line + start, 1.0, 0.0).astype(bf16)
        return dot_nn(value, chosen[: value.shape[1]])

    v.small_all[...] = placed(v.gain_rows[...], w * (width // 4)) + placed(v.bias_rows[...], w * cols)
    mask = v.mask[...].astype(f32)
    v.small_all[5:6, :] = jnp.broadcast_to(jnp.sum(mask, keepdims=True), (1, 1024))
    v.tokens_all[c] = v.tokens[...]
    meet_all()

    near_sum = SmallSum(v.small_all, v.small_near, "wa", send.take(3), recv.take(3))
    count_sum = SmallSum(v.count, v.count_far, "ctx", send.take(7), recv.take(7))
    gather = LineGather(v.tokens_all, send.take(13), recv.take(13))
    pair = [
        Columns(weight, v.pair, 128, 128 * m, send.take(4), recv.take(4), c * 128)
        for m, weight in enumerate((v.query_any, v.key_any, v.value_any, v.relative_any))
    ]
    cross = [
        Columns(weight, target, cols, first, send.take(6), recv.take(6))
        for weight, target, first in (
            (v.cross_key_any, v.pair_cols, 0),
            (v.cross_value_any, v.pair_cols, cols),
            (v.cross_query_any, v.query_cols, 0),
        )
    ]
    up_columns = Columns(v.up_any, v.up_cols, hidden, 0, send.take(6), recv.take(6))
    near_send, near_recv = send.take(3), recv.take(3)
    near_gather = GatherRows(v.near, near_send, near_recv)
    gather.start()
    near_sum.start()
    for part in pair:
        part.start()
    gather.step(0)
    near_sum.finish()
    v.count[...] = jnp.broadcast_to(v.small_all[5:6, 0:128], v.count.shape)
    count_sum.start()
    gather.step(1)
    for part in pair:
        part.finish()
    near_load.wait()
    near_gather.start()
    for part in cross:
        part.start()
    up_columns.start()
    for copy in early:
        copy.wait()
    v.table[0:seq_len, :] = dot_nn(v.waves[...], v.pair[:, 384:512]).astype(bf16)
    v.table[seq_len:, :] = jnp.zeros((TILE, 128), bf16)
    v.biases[...] = v.small_all[:, pl.ds(pl.multiple_of(c * 128, 128), 128)]
    v.gains[...] = v.small_all[:, 0:width]
    gather.step(2)
    gather.finish()
    gain_one, gain_two, gain_three = (v.gains[k : k + 1, :] for k in range(3))

    def project(part, carry):
        start = pl.multiple_of(part * tok, tok)
        value = v.tokens_all[part].astype(f32)
        normed = (value * inverse_rms(value) * gain_one).astype(bf16)
        v.normed_a[pl.ds(start, tok), :] = normed
        mixed = dot_nn(normed, v.pair[:, 0:384]).astype(bf16)
        for h in range(tok // block):
            v.qkv[part * (tok // block) + h] = mixed[h * block : (h + 1) * block]
        return carry

    lax.fori_loop(0, 8, project, 0)
    normed_out = pltpu.make_async_copy(v.normed_a, v.normed_a_any, local.take(1).at[0])
    normed_out.start()
    pair_out = pltpu.make_async_copy(v.pair_cols, v.pair_cols_any, local.take(1).at[0])
    for place in range(seq_len // block):
        take_block(v.qkv, v.inverse, place, v.qkv_order.at[place * block : (place + 1) * block, :])
    attend_tiles(v.qkv_order, v.table, v.biases[3:4, :], v.biases[4:5, :], v.heads_order)
    per = tok // block
    for place in range(seq_len // block):
        at = (place % per) * block
        take_block(v.heads_order, v.order, place, v.heads.at[place // per, at : at + block, :])
    out_swap = SwapHeads(v.heads, v.attended, True, send.take(8), recv.take(8))
    out_swap.start_out()
    near_gather.near()
    near_gather.relay()
    for part in cross:
        part.relay()
    up_columns.relay()
    for copy in late:
        copy.wait()

    gathers = [GatherRows(ref, send.take(3), recv.take(3)) for ref in (v.rows_b, v.rows_c)]
    sums = [SumRows(v.give.at[k], v.take.at[k], send.take(3), recv.take(3)) for k in range(3)]

    def output_part(r):
        return dot_nn(v.attended[r], v.output_w[...])

    out_swap.wait_rows(3)
    sums[0].give_far(output_part(3))
    out_swap.wait_rows(1)
    sums[0].give_near(output_part(1))
    out_swap.wait_rows(2)
    sums[0].pass_on(output_part(2))
    out_swap.wait_rows(0)
    v.hidden_one[...] = v.tokens[...].astype(f32) + sums[0].total(output_part(0))
    value = v.hidden_one[...]
    v.rows_b[0] = (value * inverse_rms(value) * gain_two).astype(bf16)

    gathers[0].start()
    out_swap.finish_out()
    near_gather.far()
    for part in cross:
        part.finish()
    pair_out.start()
    near_count = v.near.shape[1]

    def near_project(r, carry):
        start = pl.multiple_of(r * near_count, near_count)
        v.cross_pair[pl.ds(start, near_count), :] = dot_nn(v.near[r], v.pair_cols[...]).astype(bf16)
        return carry

    lax.fori_loop(0, 4, near_project, 0)

    def cross_part(r):
        v.cross_q[r * tok : (r + 1) * tok, :] = dot_nn(v.rows_b[r], v.query_cols[...]).astype(bf16)

        def group(g, carry):
            at = pl.multiple_of(r * tok + g * GROUP, GROUP)
            near = pl.multiple_of((r * (tok // GROUP) + g) * NK, NK)
            query = stack_all(v.cross_q[pl.ds(at, GROUP), :])
            shares = cross_shares(query, v.cross_pair[pl.ds(near, NK), 0:cols])
            out = dot_nn(shares.astype(bf16), v.cross_pair[pl.ds(near, NK), cols:])
            v.crossed[pl.ds(at, GROUP), :] = join_all(out).astype(bf16)
            return carry

        lax.fori_loop(0, tok // GROUP, group, 0)
        return dot_nn(v.crossed[r * tok : (r + 1) * tok, :], v.cross_out_w[...])

    def in_turn(gathered, summed, part, between=None):
        v.keep[0] = part(0)
        gathered.near()
        summed.give_near(part(1))
        gathered.relay()
        v.keep[2] = part(2)
        gathered.far()
        summed.give_far(part(3))
        summed.pass_on(v.keep[2])
        if between is not None:
            between()
        return summed.total(v.keep[0])

    v.hidden_two[...] = v.hidden_one[...] + in_turn(gathers[0], sums[1], cross_part)
    value = v.hidden_two[...]
    v.rows_c[0] = (value * inverse_rms(value) * gain_three).astype(bf16)

    gathers[1].start()
    up_columns.finish()

    def feed_part(r):
        part = pl.ds(r * tok, tok)
        v.pre_act[part, :] = dot_nn(v.rows_c[r], v.up_cols[...])
        v.activated[part, :] = gelu_tanh(v.pre_act[part, :]).astype(bf16)
        return dot_nn(v.activated[part, :], v.down_w[...])

    layer_out = v.hidden_two[...] + in_turn(gathers[1], sums[2], feed_part)
    v.layer_out[...] = layer_out

    count_sum.finish()
    error = layer_out - v.teacher[...].astype(f32)
    square = (tok, tok)
    same = lax.broadcasted_iota(jnp.int32, square, 0) == lax.broadcasted_iota(jnp.int32, square, 1)
    valid = jnp.sum(jnp.where(same, mask, 0.0), axis=1, keepdims=True)
    weighted = valid * error
    v.error[...] = jnp.broadcast_to(jnp.sum(weighted * error, keepdims=True), v.error.shape)
    v.out_grad[...] = (total_tokens / v.count[0:1, 0:1]) * weighted

    middle_back(v, send, recv, local, block)
    normed_out.wait()
    pair_out.wait()


def take_block(source, chosen, place, target):
    target[...] = source[chosen[place]]


def middle_back(v, send, recv, local, block):
    c, w = places_here()
    tok, width = v.tokens.shape
    rows = 4 * tok
    cols = v.output_w.shape[0]
    scale = HEAD_DIM ** (-0.5)
    first, second, third = (
        GatherRows(ref, send.take(3), recv.take(3)) for ref in (v.rows_o, v.rows_two, v.rows_one)
    )
    sum_c, sum_b = (
        SumRows(v.give.at[k], v.take.at[k], send.take(3), recv.take(3)) for k in (3, 4)
    )
    down = CtxSum(send.take(12), recv.take(12), v.down_x, v.down_half, v.down_part, v.down_share)
    up = CtxSum(send.take(12), recv.take(12), v.up_x, v.up_half, v.up_part, v.up_share)
    cross = CtxSum(
        send.take(12), recv.take(12), v.cross_x, v.cross_half, v.cross_part, v.cross_share
    )
    ctx_o = CtxSum(send.take(12), recv.take(12), v.cross_out_x, v.ctx_o_half)
    out_o = CtxSum(send.take(12), recv.take(12), v.output_x, v.out_o_half)
    heads = SwapHeads(v.heads_grad, v.heads_out, False, send.take(8), recv.take(8))
    v.rows_o[0] = v.out_grad[...].astype(bf16)

    first.start()

    def feed_back(r):
        part = pl.ds(r * tok, tok)
        act_grad = dot_nt(v.rows_o[r], v.down_w[...])
        v.pre_grad[part, :] = (act_grad * gelu_slope(v.pre_act[part, :])).astype(bf16)
        return dot_nt(v.pre_grad[part, :], v.up_cols[...])

    v.keep[0] = feed_back(0)
    first.near()
    sum_c.give_near(feed_back(1))
    first.relay()
    v.keep[1] = feed_back(2)
    first.far()
    sum_c.give_far(feed_back(3))
    sum_c.pass_on(v.keep[1])
    put_rows(v.down_x, dot_tn(v.activated[...], v.rows_o[...].reshape(rows, width)))
    down.start_y()
    put_shares(v.up_x, dot_tn(v.rows_c[...].reshape(rows, width), v.pre_grad[...]))
    up.start_y()
    normed_grad = sum_c.total(v.keep[0])
    value = v.hidden_two[...]
    inverse = inverse_rms(value)
    two_grad = v.out_grad[...] + norm_pull(value, inverse, v.gains[2:3, :], normed_grad)
    gain_three = jnp.sum(normed_grad * value * inverse, axis=0, keepdims=True)
    v.keep[1] = two_grad
    v.rows_two[0] = two_grad.astype(bf16)

    second.start()

    def cross_back(r):
        part = slice(r * tok, (r + 1) * tok)
        v.crossed_grad[...] = dot_nt(v.rows_two[r], v.cross_out_w[...]).astype(bf16)

        def group(g, carry):
            within = pl.multiple_of(g * GROUP, GROUP)
            at = pl.multiple_of(r * tok + g * GROUP, GROUP)
            near = pl.ds(pl.multiple_of((r * (tok // GROUP) + g) * NK, NK), NK)
            query = stack_all(v.cross_q[pl.ds(at, GROUP), :])
            grad = stack_all(v.crossed_grad[pl.ds(within, GROUP), :])
            keys = v.cross_pair[near, 0:cols]
            shares = cross_shares(query, keys)
            share_grad = dot_nt(grad, v.cross_pair[near, cols:])
            delta = jnp.sum(shares * share_grad, axis=1, keepdims=True)
            score_grad = (shares * (share_grad - delta)).astype(bf16)
            query_grad = join_all(dot_nn(score_grad, keys)) * scale
            v.query_grad[pl.ds(at, GROUP), :] = query_grad.astype(bf16)
            v.pair_grad[near, 0:cols] = (dot_tn(score_grad, query) * scale).astype(bf16)
            v.pair_grad[near, cols:] = dot_tn(shares.astype(bf16), grad).astype(bf16)
            return carry

        lax.fori_loop(0, tok // GROUP, group, 0)
        return dot_nt(v.query_grad[part, :], v.query_cols[...])

    v.keep[0] = cross_back(0)
    second.near()
    sum_b.give_near(cross_back(1))
    second.relay()
    v.keep[2] = cross_back(2)
    second.far()
    down.finish_y()
    down.start_z()
    sum_b.give_far(cross_back(3))
    sum_b.pass_on(v.keep[2])
    pair_grad_out = pltpu.make_async_copy(v.pair_grad, v.pair_grad_any, local.take(1).at[0])
    pair_grad_out.start()
    normed_b = v.rows_b[...].reshape(rows, width)
    put_rows(v.cross_out_x, dot_tn(v.crossed[...], v.rows_two[...].reshape(rows, width)))
    ctx_o.start_y()
    put_shares(v.cross_x, dot_tn(normed_b, v.query_grad[...]), 0)
    normed_grad = sum_b.total(v.keep[0])
    value = v.hidden_one[...]
    inverse = inverse_rms(value)
    one_grad = v.keep[1] + norm_pull(value, inverse, v.gains[1:2, :], normed_grad)
    gain_two = jnp.sum(normed_grad * value * inverse, axis=0, keepdims=True)
    v.gain_grad[...] = jnp.concatenate(
        [gain_two, gain_three, jnp.zeros((6, gain_two.shape[1]), f32)], axis=0
    )
    v.one_grad[...] = one_grad
    v.rows_one[0] = one_grad.astype(bf16)

    third.start()
    near = v.near[...].reshape(-1, width)
    put_shares(v.cross_x, dot_tn(near, v.pair_grad[...]), cols)
    cross.start_y()

    def head_back(r):
        v.heads_out[r] = dot_nt(v.rows_one[r], v.output_w[...]).astype(bf16)
        heads.start_in(r)

    head_back(0)
    third.near()
    head_back(1)
    third.relay()
    head_back(2)
    third.far()
    head_back(3)
    up.finish_y()
    up.start_z()
    attended = jnp.concatenate([v.attended[r] for r in range(4)], axis=0)
    put_rows(v.output_x, dot_tn(attended, v.rows_one[...].reshape(rows, width)))
    out_o.start_y()
    heads.finish_in()

    per = tok // block
    for place in range(8 * per):
        at = (place % per) * block
        v.heads_stored[place] = v.heads_grad[place // per, at : at + block, :]
    for place in range(8 * per):
        take_block(
            v.heads_stored, v.inverse, place, v.grad_order.at[place * block : (place + 1) * block, :]
        )

    def poll(tile):
        if tile == 1:
            down.finish_z()
        if tile == 3:
            ctx_o.finish_y()
            cross.finish_y()
            cross.start_z()
        if tile == 5:
            out_o.finish_y()
        if tile == 6:
            up.finish_z()

    content_sum, position_sum = attend_back_tiles(
        v.qkv_order,
        v.grad_order,
        v.table,
        v.biases[3:4, :],
        v.biases[4:5, :],
        v.qkv_grad_order,
        v.dkey,
        v.dvalue,
        v.drel,
        poll,
    )
    v.table_grad[...] = v.drel[0 : v.table_grad.shape[0], :] * scale
    v.bias_grad[...] = jnp.concatenate([content_sum, position_sum, jnp.zeros((6, 128), f32)], axis=0)
    for place in range(8 * per):
        at = (place % per) * block
        take_block(
            v.qkv_grad_order, v.order, place, v.query_grad_out.at[place // per, at : at + block, :]
        )
    cross.finish_z()
    pair_grad_out.wait()


def layer(total_tokens, block, orders, given, collective_id):
    tok, width = given["tokens"].shape
    hidden = given["down_any"].shape[0]
    cols = given["output_any"].shape[0]
    near = given["neighbours"].shape[0]
    seq_len = 8 * tok
    rows = 4 * tok
    padded = -(-(width // 32) // 8) * 8
    any_space = pl.BlockSpec(memory_space=pl.ANY)
    shape = jax.ShapeDtypeStruct
    vmem = pltpu.VMEM
    dma = pltpu.SemaphoreType.DMA
    results = dict(
        layer_out=shape((tok, width), f32),
        error=shape((8, 128), f32),
        count=shape((8, 128), f32),
        gains=shape((8, width), f32),
        normed_a_any=shape((seq_len, width), bf16),
        pair_cols_any=shape((width, 2 * cols), bf16),
        one_grad=shape((tok, width), f32),
        gain_grad=shape((8, width), f32),
        pair_grad_any=shape((4 * near, 2 * cols), bf16),
        query_grad_out=shape((8, tok, 384), bf16),
        table_grad=shape((seq_len, 128), f32),
        bias_grad=shape((8, 128), f32),
        down_share=shape((hidden // 8, width), bf16),
        up_share=shape((4, padded, hidden), bf16),
        cross_share=shape((4, padded, 3 * cols), bf16),
        ctx_o_half=shape((4, cols // 8, width), bf16),
        out_o_half=shape((4, cols // 8, width), bf16),
    )
    scratch = dict(
        small_all=vmem((8, 1024), f32),
        small_near=vmem((3, 8, 1024), f32),
        qkv=vmem((seq_len // block, block, 384), bf16),
        table=vmem((seq_len + TILE, 128), bf16),
        biases=vmem((8, 128), f32),
        normed_a=vmem((seq_len, width), bf16),
        pair_cols=vmem((width, 2 * cols), bf16),
        heads_grad=vmem((8, tok, 128), bf16),
        grad_order=vmem((seq_len, 128), bf16),
        pair_grad=vmem((4 * near, 2 * cols), bf16),
        qkv_grad_order=vmem((seq_len // block, block, 384), bf16),
        dkey=vmem((seq_len, 128), f32),
        dvalue=vmem((seq_len, 128), f32),
        drel=vmem((seq_len + TILE, 128), f32),
        cross_half=vmem((4, 4, padded, 3 * cols), bf16),
        cross_part=vmem((3, 4, padded, 3 * cols), bf16),
        cross_out_x=vmem((4, 2, cols // 8, width), bf16),
        output_x=vmem((4, 2, cols // 8, width), bf16),
        count_far=vmem((7, 8, 128), f32),
        tokens_all=vmem((8, tok, width), bf16),
        pair=vmem((width, 512), bf16),
        waves=vmem((seq_len, width), bf16),
        qkv_order=vmem((seq_len, 384), bf16),
        heads_order=vmem((seq_len // block, block, 128), bf16),
        heads_stored=vmem((seq_len // block, block, 128), bf16),
        heads=vmem((8, tok, 128), bf16),
        attended=vmem((4, tok, cols), bf16),
        near=vmem((4, near, width), bf16),
        query_cols=vmem((width, cols), bf16),
        up_cols=vmem((width, hidden), bf16),
        output_w=vmem((cols, width), bf16),
        cross_out_w=vmem((cols, width), bf16),
        down_w=vmem((hidden, width), bf16),
        cross_pair=vmem((4 * near, 2 * cols), bf16),
        cross_q=vmem((rows, cols), bf16),
        crossed=vmem((rows, cols), bf16),
        crossed_grad=vmem((tok, cols), bf16),
        hidden_one=vmem((tok, width), f32),
        hidden_two=vmem((tok, width), f32),
        out_grad=vmem((tok, width), f32),
        pre_act=vmem((rows, hidden), f32),
        activated=vmem((rows, hidden), bf16),
        rows_b=vmem((4, tok, width), bf16),
        rows_c=vmem((4, tok, width), bf16),
        rows_o=vmem((4, tok, width), bf16),
        rows_two=vmem((4, tok, width), bf16),
        rows_one=vmem((4, tok, width), bf16),
        give=vmem((5, 3, tok, width), bf16),
        take=vmem((5, 3, tok, width), bf16),
        keep=vmem((3, tok, width), f32),
        pre_grad=vmem((rows, hidden), bf16),
        query_grad=vmem((rows, cols), bf16),
        heads_out=vmem((4, tok, cols), bf16),
        down_x=vmem((4, 2, hidden // 8, width), bf16),
        down_half=vmem((4, hidden // 8, width), bf16),
        down_part=vmem((3, hidden // 8, width), bf16),
        up_x=vmem((4, 2, 4, padded, hidden), bf16),
        up_half=vmem((4, 4, padded, hidden), bf16),
        up_part=vmem((3, 4, padded, hidden), bf16),
        cross_x=vmem((4, 2, 4, padded, 3 * cols), bf16),
        send=dma((232,)),
        recv=dma((232,)),
        local=dma((8,)),
    )
    names = [*orders, *given, *results, *scratch]
    specs = [in_smem] * len(orders) + [
        any_space if name.endswith("_any") or name == "neighbours" else in_vmem for name in given
    ]
    got = pl.pallas_call(
        functools.partial(layer_kernel, names, total_tokens, block),
        out_shape=list(results.values()),
        in_specs=specs,
        out_specs=[any_space if name.endswith("_any") else in_vmem for name in results],
        scratch_shapes=list(scratch.values()),
        compiler_params=pltpu.CompilerParams(
            collective_id=collective_id, has_side_effects=True, vmem_limit_bytes=62 * 2**20
        ),
        name="layer",
    )(*orders.values(), *given.values())
    return types.SimpleNamespace(**dict(zip(results, got, strict=True)))


class Spread:

    def __init__(self, share, out, send, recv):
        self.share, self.out, self.send, self.recv = share, out, send, recv
        self.c, self.w = places_here()

    def columns(self, place):
        width = self.share.shape[2]
        return self.out.at[self.c, :, pl.ds(pl.multiple_of(place * width, 128), width)]

    def copy(self, j, place):
        return remote(
            self.share.at[self.w ^ j],
            self.columns(place),
            self.send.at[j],
            self.recv.at[j],
            self.c,
            self.w ^ j,
        )

    def own(self):
        return pltpu.make_async_copy(
            self.share.at[self.w], self.columns(self.w), self.send.at[0]
        )

    def start(self):
        for j in (2, 3, 1):
            self.copy(j, self.w).start()
        self.own().start()

    def finish(self):
        self.own().wait()
        for j in (1, 2, 3):
            self.copy(j, self.w).wait_send()
            self.copy(j, self.w ^ j).wait_recv()


class Whole:

    def __init__(self, source, target, send, recv):
        self.source, self.target, self.send, self.recv = source, target, send, recv
        self.c, self.w = places_here()

    def put(self, place):
        rows = self.source.shape[0]
        return self.target.at[pl.ds(pl.multiple_of(place * rows, 32), rows), :]

    def copy(self, j, place):
        return remote(
            self.source, self.put(place), self.send.at[j], self.recv.at[j], self.c, self.w ^ j
        )

    def passed(self, place):
        ref = self.put(place)
        return remote(ref, ref, self.send.at[3], self.recv.at[3], self.c, self.w ^ 1)

    def own(self):
        return pltpu.make_async_copy(self.source, self.put(self.w), self.send.at[0])

    def start(self):
        self.copy(2, self.w).start()
        self.copy(1, self.w).start()
        self.own().start()

    def relay(self):
        self.copy(2, self.w).wait_send()
        self.copy(2, self.w ^ 2).wait_recv()
        self.passed(self.w ^ 2).start()

    def finish(self):
        self.own().wait()
        self.copy(1, self.w).wait_send()
        self.copy(1, self.w ^ 1).wait_recv()
        self.passed(self.w ^ 2).wait_send()
        self.passed(self.w ^ 3).wait_recv()


class MaskSum:

    def __init__(self, ref, got, masks, send, recv):
        self.ref, self.got, self.masks, self.send, self.recv = ref, got, masks, send, recv
        self.c, self.w = places_here()

    def copy(self, k):
        ctx, wa = self.masks[k]
        return remote(
            self.ref, self.got.at[k], self.send.at[k], self.recv.at[k], self.c ^ ctx, self.w ^ wa
        )

    def start(self):
        for k in range(len(self.masks)):
            self.copy(k).start()

    def finish(self):
        for k in range(len(self.masks)):
            self.copy(k).wait()
        self.ref[...] = tree_sum([self.ref[...]] + [self.got[k] for k in range(len(self.masks))])


def finish_kernel(names, *refs):
    v = types.SimpleNamespace(**dict(zip(names, refs, strict=True)))
    c, w = places_here()
    send, recv, local = Pool(v.send), Pool(v.recv), Pool(v.local)
    tok, width = v.tokens.shape
    cols = v.out_o_half.shape[1] * 8
    share = width // 4

    def load(source, target):
        copy = pltpu.make_async_copy(source, target, local.take(1).at[0])
        copy.start()
        return copy

    loads = [load(v.normed_a_any, v.normed_a), load(v.waves_any, v.waves)]
    late = [load(v.pair_cols_any, v.pair_cols), load(v.near_any, v.near_rows)]

    def line(out):
        return LineGather(out, send.take(13), recv.take(13))

    def summed(x, half, part, got):
        return CtxSum(send.take(12), recv.take(12), x, half, part, got)

    down, up, cross, ctx_o, out_o, pair = (
        line(out)
        for out in (v.down_out, v.up_all, v.cross_all, v.cross_o_out, v.output_out, v.pair_all)
    )
    ctx_o_sum = summed(None, v.ctx_o_half, v.ctx_o_part, v.ctx_o_share)
    out_o_sum = summed(None, v.out_o_half, v.out_o_part, v.out_o_share)
    up_spread = Spread(v.up_share, v.up_all, send.take(4), recv.take(4))
    cross_spread = Spread(v.cross_share, v.cross_all, send.take(4), recv.take(4))
    sum_pair = SumRows(v.pair_give, v.pair_take, send.take(3), recv.take(3))
    sum_near = SumRows(v.near_give, v.near_take, send.take(3), recv.take(3))
    weights = [
        Whole(weight, v.full.at[m], send.take(4), recv.take(4))
        for m, weight in enumerate((v.query_any, v.key_any, v.value_any))
    ]
    stages = [
        MaskSum(v.total, got, masks, send.take(3), recv.take(3))
        for got, masks in (
            (v.got_wa, ((0, 1), (0, 2), (0, 3))),
            (v.got_y, ((1, 0),)),
            (v.got_z, ((2, 0), (4, 0), (6, 0))),
        )
    ]
    b_send, b_recv = send.take(24), recv.take(24)

    def block_copy(j, m, place):
        return remote(
            v.query_grad.at[c ^ j, :, 128 * m : 128 * (m + 1)],
            v.mine.at[m, :, pl.ds(pl.multiple_of(place * 128, 128), 128)],
            b_send.at[3 * j + m],
            b_recv.at[3 * j + m],
            c ^ j,
            w,
        )

    own_blocks = [
        pltpu.make_async_copy(
            v.query_grad.at[c, :, 128 * m : 128 * (m + 1)],
            v.mine.at[m, :, pl.ds(pl.multiple_of(c * 128, 128), 128)],
            b_recv.at[m],
        )
        for m in range(3)
    ]
    v.down_out[c] = v.down_share[...]
    meet_lines()
    up_spread.start()
    cross_spread.start()
    down.start()
    ctx_o_sum.start_z()
    out_o_sum.start_z()
    for copy in own_blocks:
        copy.start()

    query_grad = v.query_grad[...].reshape(-1, v.query_grad.shape[2])
    high = v.table_grad[...].astype(bf16)
    low = (v.table_grad[...] - high.astype(f32)).astype(bf16)
    for copy in loads:
        copy.wait()
    mixed = dot_tn(v.normed_a[...], query_grad)
    turned = dot_tn(v.waves[...], high) + dot_tn(v.waves[...], low)
    for place in range(4):
        at = place * share
        v.sums[place] = jnp.concatenate([mixed[at : at + share], turned[at : at + share]], axis=1)
    sum_pair.give_far(v.sums[w ^ 3])
    sum_pair.give_near(v.sums[w ^ 1])
    up_spread.finish()
    up.start()
    cross_spread.finish()
    cross.start()
    sum_pair.pass_on(v.sums[w ^ 2])
    down.step(0)
    for j in (4, 6, 5, 7, 2, 3, 1):
        for m in range(3):
            block_copy(j, m, c).start()
    v.pair_all[c] = sum_pair.total(v.sums[w]).astype(bf16)
    pair.start()
    for copy in late:
        copy.wait()
    near_count = v.near_grad.shape[0]

    def near_part(r):
        return dot_nt(v.near_rows[r * near_count : (r + 1) * near_count, :], v.pair_cols[...])

    sum_near.give_far(near_part(3))
    sum_near.give_near(near_part(1))
    sum_near.pass_on(near_part(2))
    for weight in weights:
        weight.start()
    v.near_grad[...] = near_part(0)
    up.step(0)
    down.step(1)
    cross.step(0)
    ctx_o_sum.finish_z()
    v.cross_o_out[c] = v.ctx_o_share[...]
    ctx_o.start()
    out_o_sum.finish_z()
    v.output_out[c] = v.out_o_share[...]
    out_o.start()
    up.step(1)
    cross.step(1)
    pair.step(0)
    down.step(2)
    ctx_o.step(0)
    out_o.step(0)
    up.step(2)
    cross.step(2)
    pair.step(1)
    ctx_o.step(1)
    out_o.step(1)

    for j in range(1, 8):
        for m in range(3):
            block_copy(j, m, c ^ j).wait_recv()
    for copy in own_blocks:
        copy.wait()
    pair.step(2)
    for weight in weights:
        weight.relay()
    for weight in weights:
        weight.finish()
    normed_grad = dot_nt(v.mine[0], v.full[0])
    normed_grad = normed_grad + dot_nt(v.mine[1], v.full[1])
    normed_grad = normed_grad + dot_nt(v.mine[2], v.full[2])
    hidden = v.tokens[...].astype(f32)
    inverse = inverse_rms(hidden)
    v.tokens_grad[...] = v.one_grad[...] + norm_pull(hidden, inverse, v.gains[0:1, :], normed_grad)
    v.total[...] = v.small[...]
    v.total[0:1, 0:width] = jnp.sum(normed_grad * hidden * inverse, axis=0, keepdims=True)
    stages[0].start()
    ctx_o.step(2)
    out_o.step(2)
    stages[0].finish()
    stages[1].start()
    v.near_grad[...] = sum_near.total(v.near_grad[...])
    stages[1].finish()
    stages[2].start()
    down.finish()
    up.finish()
    used = share // 8

    def lay_up(part, at):
        v.up_out[at : at + used, :] = v.up_all[part, 0:used, :].astype(f32)

    for part in range(8):
        lay_up(part, part * used)
    pair.finish()
    for part in range(8):
        for m in range(4):
            v.pair_out[m, :, 128 * part : 128 * (part + 1)] = v.pair_all[
                part, :, 128 * m : 128 * (m + 1)
            ]
    ctx_o.finish()
    out_o.finish()
    cross.finish()
    for part in range(8):
        for m in range(3):
            for place in range(4):
                at = (place * 3 + m) * cols
                v.cross_out[m, part * used : (part + 1) * used, place * cols : (place + 1) * cols] = (
                    v.cross_all[part, 0:used, at : at + cols].astype(f32)
                )
    stages[2].finish()
    for j in range(1, 8):
        for m in range(3):
            block_copy(j, m, c).wait_send()


def finish(given, collective_id):
    tok, width = given["tokens"].shape
    near = given["near_any"].shape[0]
    padded = given["up_share"].shape[1]
    hidden = given["up_share"].shape[2]
    cols = given["out_o_half"].shape[1] * 8
    share = width // 4
    any_space = pl.BlockSpec(memory_space=pl.ANY)
    shape = jax.ShapeDtypeStruct
    vmem = pltpu.VMEM
    dma = pltpu.SemaphoreType.DMA
    part = (cols // 8, width)
    results = dict(
        tokens_grad=shape((tok, width), f32),
        near_grad=shape((near // 4, width), f32),
        total=shape(given["small"].shape, f32),
        down_out=shape((8,) + given["down_share"].shape, bf16),
        up_out=shape((share, 4 * hidden), f32),
        cross_out=shape((3, share, 4 * cols), f32),
        cross_o_out=shape((8,) + part, bf16),
        output_out=shape((8,) + part, bf16),
        pair_out=shape((4, share, 1024), bf16),
    )
    scratch = dict(
        normed_a=vmem(given["normed_a_any"].shape, bf16),
        waves=vmem(given["waves_any"].shape, bf16),
        pair_cols=vmem(given["pair_cols_any"].shape, bf16),
        near_rows=vmem(given["near_any"].shape, bf16),
        full=vmem((3, width, 1024), bf16),
        mine=vmem((3, tok, 1024), bf16),
        sums=vmem((4, share, 512), f32),
        up_all=vmem((8, padded, 4 * hidden), bf16),
        cross_all=vmem((8, padded, 12 * cols), bf16),
        pair_all=vmem((8, share, 512), bf16),
        ctx_o_part=vmem((3,) + part, bf16),
        ctx_o_share=vmem(part, bf16),
        out_o_part=vmem((3,) + part, bf16),
        out_o_share=vmem(part, bf16),
        pair_give=vmem((3, share, 512), bf16),
        pair_take=vmem((3, share, 512), bf16),
        near_give=vmem((3, near // 4, width), bf16),
        near_take=vmem((3, near // 4, width), bf16),
        got_wa=vmem((3,) + given["small"].shape, f32),
        got_y=vmem((1,) + given["small"].shape, f32),
        got_z=vmem((3,) + given["small"].shape, f32),
        send=dma((184,)),
        recv=dma((184,)),
        local=dma((4,)),
    )
    names = [*given, *results, *scratch]
    got = pl.pallas_call(
        functools.partial(finish_kernel, names),
        out_shape=list(results.values()),
        in_specs=[any_space if name.endswith("_any") else in_vmem for name in given],
        out_specs=[in_vmem] * len(results),
        scratch_shapes=list(scratch.values()),
        compiler_params=pltpu.CompilerParams(
            collective_id=collective_id, has_side_effects=True, vmem_limit_bytes=62 * 2**20
        ),
        name="finish",
    )(*given.values())
    return types.SimpleNamespace(**dict(zip(results, got, strict=True)))


def skew(wide, count):
    lead = wide.shape[:-2]
    rows, span = wide.shape[-2:]
    edge = [(0, 0)] * len(lead)
    padded = jnp.pad(wide, edge + [(0, 0), (0, 1)])
    flat = padded.reshape(lead + (rows * (span + 1),))
    flat = lax.slice_in_dim(flat, rows - 1, rows - 1 + rows * span, axis=len(lead))
    return flat.reshape(lead + (rows, span))[..., :count]


def unskew(grad, span):
    lead = grad.shape[:-2]
    rows, count = grad.shape[-2:]
    edge = [(0, 0)] * len(lead)
    wide = jnp.pad(grad, edge + [(0, 0), (0, span - count)])
    flat = jnp.pad(wide.reshape(lead + (rows * span,)), edge + [(rows - 1, 1)])
    return flat.reshape(lead + (rows, span + 1))[..., :span]


def tile_scores(content_rows, position_rows, key_rows, relative, row_start, key_start):
    rows = content_rows.shape[0]
    count = key_rows.shape[0]
    scale = content_rows.shape[-1] ** (-0.5)
    content = jnp.einsum("qhe,khe->hqk", content_rows, key_rows, preferred_element_type=f32)
    wide = jnp.einsum("qhe,whe->hqw", position_rows, relative, preferred_element_type=f32)
    scores = (content + skew(wide, count)) * scale
    causal = (row_start + jnp.arange(rows))[:, None] >= (key_start + jnp.arange(count))[None, :]
    return (scores, causal[None])


def tile_forward(
    content_rows, position_rows, row_start, relative, key_rows, value_rows, key_start, state
):
    top, total, accum = state
    scores, causal = tile_scores(
        content_rows, position_rows, key_rows, relative, row_start, key_start
    )
    scores = jnp.where(causal, scores, neg_big)
    new_top = jnp.maximum(top, jnp.max(scores, axis=-1))
    raised = jnp.where(causal, jnp.exp(scores - new_top[..., None]), 0.0)
    fade = jnp.exp(top - new_top)
    total = total * fade + jnp.sum(raised, axis=-1)
    accum = accum * fade[..., None] + jnp.einsum(
        "hqk,khe->hqe", raised.astype(bf16), value_rows, preferred_element_type=f32
    )
    return (new_top, total, accum)


def tile_backward(
    content_rows,
    position_rows,
    row_start,
    relative,
    key_rows,
    value_rows,
    grad_rows,
    log_rows,
    delta_rows,
    key_start,
):
    scores, causal = tile_scores(
        content_rows, position_rows, key_rows, relative, row_start, key_start
    )
    scale = content_rows.shape[-1] ** (-0.5)
    shares = jnp.where(causal, jnp.exp(scores - log_rows[..., None]), 0.0)
    share_grad = jnp.einsum("qhe,khe->hqk", grad_rows, value_rows, preferred_element_type=f32)
    score_grad = (shares * (share_grad - delta_rows[..., None])).astype(bf16)
    content_grad = jnp.einsum("hqk,khe->qhe", score_grad, key_rows, preferred_element_type=f32)
    wide_grad = unskew(score_grad, relative.shape[0])
    position_grad = jnp.einsum("hqw,whe->qhe", wide_grad, relative, preferred_element_type=f32)
    table_part = jnp.einsum("hqw,qhe->whe", wide_grad, position_rows, preferred_element_type=f32)
    key_grad = jnp.einsum("hqk,qhe->khe", score_grad, content_rows, preferred_element_type=f32)
    value_grad = jnp.einsum(
        "hqk,qhe->khe", shares.astype(bf16), grad_rows, preferred_element_type=f32
    )
    return (
        content_grad * scale,
        position_grad * scale,
        table_part * scale,
        key_grad * scale,
        value_grad,
    )


def nest_tiles(tile_fn):
    inner = jax.vmap(tile_fn, in_axes=(0, 0, 0, 0, None, None, 0))
    return jax.vmap(inner, in_axes=(0, 0, None, None, 0, 0, 0))


def to_global(stored, inverse, block):
    seqs, seq_len, width = stored.shape
    blocks = stored.reshape(seqs, seq_len // block, block * width)
    chosen = (inverse[:, None] == jnp.arange(seq_len // block)[None, :]).astype(bf16)
    moved = jnp.einsum("gs,nsx->ngx", chosen, blocks, preferred_element_type=f32)
    return moved.astype(bf16).reshape(stored.shape)


class SplitQueries:

    def __init__(self, query, keys, values, biases, relative, block_order, inverse, block):
        self.seqs, self.tok_dev, self.width = keys.shape
        self.heads = self.width // HEAD_DIM
        self.block = block
        self.block_order = block_order
        ctx_count = lax.axis_size("ctx")
        self.seq_len = self.tok_dev * ctx_count
        self.key_len = min(512, self.seq_len)
        pad = jnp.zeros((self.key_len + block, self.width), bf16)
        table = jnp.concatenate([relative, pad], axis=0)
        self.table = table.reshape(-1, self.heads, HEAD_DIM)
        lead = (self.seqs, 2, block, self.heads, HEAD_DIM)
        self.content = (query + biases[0]).astype(bf16).reshape(lead)
        self.position = (query + biases[1]).astype(bf16).reshape(lead)
        gathered = [lax.all_gather(part, "ctx", axis=1, tiled=True) for part in (keys, values)]
        shape = (self.seqs, self.seq_len, self.heads, HEAD_DIM)
        self.keys, self.values = [to_global(part, inverse, block).reshape(shape) for part in gathered]
        self.starts = lax.dynamic_slice_in_dim(block_order, 2 * lax.axis_index("ctx"), 2, 0) * block

    def rows(self, index):
        start = index * self.key_len
        keys = lax.dynamic_slice_in_dim(self.keys, start, self.key_len, 1)
        values = lax.dynamic_slice_in_dim(self.values, start, self.key_len, 1)
        span = self.block + self.key_len
        offsets = [self.seq_len - self.block - self.starts[slot] + start for slot in range(2)]
        relative = [lax.dynamic_slice_in_dim(self.table, offset, span, 0) for offset in offsets]
        return start, keys, values, jnp.stack(relative), offsets

    def to_stored(self, part):
        count = self.seq_len // self.block
        blocks = part.reshape(self.seqs, count, self.block * self.width)
        chosen = (self.block_order[:, None] == jnp.arange(count)[None, :]).astype(f32)
        moved = jnp.einsum("sg,ngx->nsx", chosen, blocks, precision=highest)
        return moved.reshape(self.seqs, self.seq_len, self.width)

    def forward(self):
        def step(state, index):
            start, keys, values, relative, _ = self.rows(index)

            def tile(content, position, row_start, table, keys_seq, values_seq, tile_state):
                return tile_forward(
                    content, position, row_start, table, keys_seq, values_seq, start, tile_state
                )

            return nest_tiles(tile)(
                self.content, self.position, self.starts, relative, keys, values, state
            ), None

        shape = (self.seqs, 2, self.heads, self.block)
        state = (
            jnp.full(shape, neg_big, f32),
            jnp.zeros(shape, f32),
            jnp.zeros(shape + (HEAD_DIM,), f32),
        )
        (top, total, accum), _ = lax.scan(step, state, jnp.arange(self.seq_len // self.key_len))
        self.log_total = top + jnp.log(total)
        self.out = accum / total[..., None]
        moved = jnp.transpose(self.out, (0, 1, 3, 2, 4))
        return moved.reshape(self.seqs * self.tok_dev, self.width).astype(bf16)

    def backward(self, grad):
        block, seq_len, key_len = self.block, self.seq_len, self.key_len
        lead = (self.seqs, 2, block, self.heads, HEAD_DIM)
        grad = grad.reshape(lead)
        delta = jnp.einsum("sbqhe,sbhqe->sbhq", grad.astype(f32), self.out)
        def step(carry, index):
            start, keys, values, relative, offsets = self.rows(index)

            def tile(content, position, row_start, table, keys_seq, values_seq, extra):
                return tile_backward(
                    content, position, row_start, table, keys_seq, values_seq, *extra, start
                )

            extra = (grad, self.log_total, delta)
            parts = nest_tiles(tile)(
                self.content, self.position, self.starts, relative, keys, values, extra
            )
            table = carry[2]
            table_sum = jnp.sum(parts[2], axis=0)
            for slot in range(2):
                offset = offsets[slot]
                current = lax.dynamic_slice_in_dim(table, offset, block + key_len, 0)
                table = lax.dynamic_update_slice_in_dim(table, current + table_sum[slot], offset, 0)
            sums = []
            for total, part in zip(carry[3:], parts[3:]):
                current = lax.dynamic_slice_in_dim(total, start, key_len, 1)
                part = current + jnp.sum(part, axis=1)
                sums.append(lax.dynamic_update_slice_in_dim(total, part, start, 1))
            key_acc, value_acc = sums
            return (carry[0] + parts[0], carry[1] + parts[1], table, key_acc, value_acc), None

        zero_tiles = jnp.zeros(lead, f32)
        zero_keys = jnp.zeros((self.seqs, seq_len, self.heads, HEAD_DIM), f32)
        carry = (zero_tiles, zero_tiles, jnp.zeros(self.table.shape, f32), zero_keys, zero_keys)
        carry, _ = lax.scan(step, carry, jnp.arange(seq_len // key_len))
        owned = [
            lax.psum_scatter(
                self.to_stored(part), "ctx", scatter_dimension=1, tiled=True
            )
            for part in carry[3:]
        ]
        flat = (self.seqs * self.tok_dev, self.width)
        query_grad = (carry[0] + carry[1]).reshape(flat).astype(bf16)
        key_grad, value_grad = [part.reshape(flat).astype(bf16) for part in owned]
        bias_grads = jnp.stack(
            [jnp.sum(part, axis=(0, 1, 2)).reshape(self.width) for part in carry[:2]]
        )
        table_grad = carry[2].reshape(-1, self.width)[:seq_len]
        return query_grad, key_grad, value_grad, bias_grads, table_grad


def local_general(
    tokens,
    neighbours,
    teacher,
    valid_mask,
    block_order,
    query_weight,
    key_weight,
    value_weight,
    output_weight,
    relative_weight,
    content_bias,
    position_bias,
    cross_query_weight,
    cross_key_weight,
    cross_value_weight,
    cross_output_weight,
    up_weight,
    down_weight,
    attention_gain,
    cross_gain,
    feedforward_gain,
):
    places = lax.axis_size("wa")
    ctx_count = lax.axis_size("ctx")
    place = lax.axis_index("wa")
    here = lax.axis_index("ctx")
    _, tok_dev, width = tokens.shape
    seq_len = tok_dev * ctx_count
    block = tok_dev // 2
    cols = HEADS * HEAD_DIM // places
    rows = places * tok_dev

    token_parts = gather_parts(tokens[0])
    query_cols, key_cols, value_cols = [
        take_columns(weight) for weight in (query_weight, key_weight, value_weight)
    ]
    relative_cols = take_columns(relative_weight)
    gains = lax.all_gather(
        jnp.stack([attention_gain, cross_gain, feedforward_gain]), "wa", axis=1, tiled=True
    ).astype(f32)
    gain_one, gain_two, gain_three = gains[0:1], gains[1:2], gains[2:3]
    cross_query_cols, cross_key_cols, cross_value_cols = [
        take_columns(weight) for weight in (cross_query_weight, cross_key_weight, cross_value_weight)
    ]
    cross_pair_cols = jnp.concatenate([cross_key_cols, cross_value_cols], axis=1)
    near_rows = jnp.concatenate(gather_parts(neighbours.reshape(-1, width)), axis=0)
    up_cols = take_columns(up_weight)
    valid = valid_mask.astype(f32).reshape(tok_dev, 1)
    count = jnp.sum(valid).reshape(1, 1)
    count = all_summed(all_summed(count, "wa"), "ctx")

    slots = jnp.arange(2 * ctx_count)
    inverse = jnp.sum(jnp.where(block_order[None, :] == slots[:, None], slots[None, :], 0), axis=1)
    inverse = inverse.astype(jnp.int32)
    distance = (seq_len - 1 - jnp.arange(seq_len)).astype(f32)
    waves = sinusoid(distance, width).astype(bf16)

    hidden_all = jnp.concatenate(token_parts, axis=0).astype(f32)
    scale_all = inverse_rms(hidden_all)
    normed_a = (hidden_all * scale_all * gain_one).astype(bf16)
    biases = jnp.stack([content_bias, position_bias]).astype(f32)
    mixed_cols = jnp.concatenate([query_cols, key_cols, value_cols], axis=1)
    qkv = dot_nn(normed_a, mixed_cols).reshape(places, tok_dev, 3 * cols)
    relative = dot_nn(waves, relative_cols).astype(bf16)
    general = SplitQueries(
        qkv[..., :cols],
        qkv[..., cols : 2 * cols].astype(bf16),
        qkv[..., 2 * cols :].astype(bf16),
        biases,
        relative,
        block_order,
        inverse,
        block,
    )
    attended = general.forward()

    def to_owner(product):
        return scatter_parts([product[r * tok_dev : (r + 1) * tok_dev] for r in range(places)])

    def from_all(value):
        return jnp.concatenate(gather_parts(value), axis=0)

    hidden_in = tokens[0].astype(f32)
    hidden_one = hidden_in + to_owner(dot_nn(attended, output_weight))

    scale_two = inverse_rms(hidden_one)
    normed_b = from_all((hidden_one * scale_two * gain_two).astype(bf16))
    cross_q = dot_nn(normed_b, cross_query_cols).astype(bf16)
    cross_pair = dot_nn(near_rows, cross_pair_cols).astype(bf16)
    crossed = cross_forward(cross_q, cross_pair)
    hidden_two = hidden_one + to_owner(dot_nn(crossed, cross_output_weight))

    scale_three = inverse_rms(hidden_two)
    normed_c = from_all((hidden_two * scale_three * gain_three).astype(bf16))
    pre_act = dot_nn(normed_c, up_cols)
    activated = gelu_tanh(pre_act).astype(bf16)
    layer_out = hidden_two + to_owner(dot_nn(activated, down_weight))

    error = layer_out - teacher[0].astype(f32)
    error_sum = jnp.sum(valid * error * error).reshape(1, 1)
    error_sum = all_summed(all_summed(error_sum, "wa"), "ctx")
    loss = (error_sum / (2.0 * count * width)).reshape(())
    out_grad = (places * seq_len) / count * valid * error

    out_low = from_all(out_grad.astype(bf16))
    act_grad = dot_nt(out_low, down_weight)
    _, gelu_pull = jax.vjp(gelu_tanh, pre_act)
    pre_grad = gelu_pull(act_grad)[0].astype(bf16)
    down_grad = dot_tn(activated, out_low).astype(bf16)
    up_grad = dot_tn(normed_c, pre_grad).astype(bf16)
    normed_c_grad = to_owner(dot_nt(pre_grad, up_cols))
    two_grad = out_grad + norm_pull(hidden_two, scale_three, gain_three, normed_c_grad)
    gain_three_grad = jnp.sum(normed_c_grad * hidden_two * scale_three, axis=0, keepdims=True)
    down_out = sum_row_grads(down_grad)
    up_out = sum_column_grads(up_grad[None])[0]

    two_low = from_all(two_grad.astype(bf16))
    crossed_grad = dot_nt(two_low, cross_output_weight).astype(bf16)
    cross_q_grad, cross_pair_grad = cross_backward(cross_q, cross_pair, crossed_grad)
    normed_b_grad = to_owner(dot_nt(cross_q_grad, cross_query_cols))
    one_grad = two_grad + norm_pull(hidden_one, scale_two, gain_two, normed_b_grad)
    gain_two_grad = jnp.sum(normed_b_grad * hidden_one * scale_two, axis=0, keepdims=True)
    cross_output_grad = dot_tn(crossed, two_low).astype(bf16)
    cross_query_grad = dot_tn(normed_b, cross_q_grad).astype(bf16)
    cross_key_grad = dot_tn(near_rows, cross_pair_grad[:, :cols]).astype(bf16)
    cross_value_grad = dot_tn(near_rows, cross_pair_grad[:, cols:]).astype(bf16)
    cross_output_out = sum_row_grads(cross_output_grad)
    cross_out = sum_column_grads(jnp.stack([cross_key_grad, cross_value_grad]))
    cross_query_out = sum_column_grads(cross_query_grad[None])[0]
    near_grad = dot_nt(cross_pair_grad, cross_pair_cols)
    near_count = near_rows.shape[0] // places
    near_grad = scatter_parts(
        [near_grad[r * near_count : (r + 1) * near_count] for r in range(places)]
    )
    neighbours_grad = near_grad.reshape(neighbours.shape)

    one_low = from_all(one_grad.astype(bf16))
    attended_grad = dot_nt(one_low, output_weight).astype(bf16)
    output_grad = dot_tn(attended, one_low).astype(bf16)
    output_out = sum_row_grads(output_grad)
    query_grad, key_grad, value_grad, bias_grads, table_grad = general.backward(attended_grad)
    qkv_grad = jnp.concatenate([query_grad, key_grad, value_grad], axis=1)
    table_high = table_grad.astype(bf16)
    table_low = (table_grad - table_high.astype(f32)).astype(bf16)
    relative_grad = (dot_tn(waves, table_high) + dot_tn(waves, table_low)).astype(bf16)
    mixed_grad = dot_tn(normed_a, qkv_grad).astype(bf16)
    whole = [mixed_grad[:, m * cols : (m + 1) * cols] for m in range(3)]
    attention_out = sum_column_grads(jnp.stack(whole + [relative_grad]))
    normed_a_part = dot_nt(qkv_grad, mixed_cols)
    gain_one_part = jnp.sum(normed_a_part * hidden_all * scale_all, axis=0, keepdims=True)
    normed_a_grad = to_owner(normed_a_part)
    tokens_grad = one_grad + norm_pull(hidden_in, scale_all[:tok_dev], gain_one, normed_a_grad)

    gain_grads = jnp.concatenate([gain_one_part, gain_two_grad, gain_three_grad], axis=0)
    gain_grads = all_summed(gain_grads, "wa")
    share = width // places
    gain_grads = lax.dynamic_slice_in_dim(gain_grads, place * share, share, 1)
    small = jnp.concatenate([gain_grads.reshape(1, -1), bias_grads.reshape(1, -1)], axis=1)
    small = all_summed(small, "ctx")[0]
    gain_out = small[: 3 * share].reshape(3, share)
    bias_out = small[3 * share :].reshape(2, cols)

    return (
        layer_out[None],
        loss,
        tokens_grad[None],
        neighbours_grad,
        attention_out[0],
        attention_out[1],
        attention_out[2],
        output_out,
        attention_out[3],
        bias_out[0],
        bias_out[1],
        cross_query_out,
        cross_out[0],
        cross_out[1],
        cross_output_out,
        up_out,
        down_out,
        gain_out[0],
        gain_out[1],
        gain_out[2],
    )


def local_by_heads(
    tokens,
    neighbours,
    teacher,
    valid_mask,
    block_order,
    query_weight,
    key_weight,
    value_weight,
    output_weight,
    relative_weight,
    content_bias,
    position_bias,
    cross_query_weight,
    cross_key_weight,
    cross_value_weight,
    cross_output_weight,
    up_weight,
    down_weight,
    attention_gain,
    cross_gain,
    feedforward_gain,
):
    places = 4
    ctx_count = 8
    place = lax.axis_index("wa")
    here = lax.axis_index("ctx")
    _, tok_dev, width = tokens.shape
    seq_len = tok_dev * ctx_count
    block = tok_dev // 2
    attn = HEADS * HEAD_DIM
    cols = attn // places
    share = width // places

    slots = jnp.arange(2 * ctx_count)
    inverse = jnp.sum(jnp.where(block_order[None, :] == slots[:, None], slots[None, :], 0), axis=1)
    inverse = inverse.astype(jnp.int32)
    gain_rows = jnp.concatenate(
        [jnp.stack([attention_gain, cross_gain, feedforward_gain]), jnp.zeros((5, share), bf16)]
    )
    blank = jnp.zeros((3, cols), bf16)
    bias_rows = jnp.concatenate([blank, content_bias[None], position_bias[None], blank])

    half = width // 2
    freq = jnp.exp(-jnp.log(10000.0) * jnp.arange(half, dtype=f32) * 2.0 / width)
    coarse = (64.0 * jnp.arange(seq_len // 64, dtype=f32)[::-1])[:, None] * freq
    fine = jnp.arange(64, dtype=f32)[::-1][:, None] * freq
    sin_a, cos_a = jnp.sin(coarse)[:, None], jnp.cos(coarse)[:, None]
    sin_b, cos_b = jnp.sin(fine)[None], jnp.cos(fine)[None]
    waves = jnp.concatenate(
        [sin_a * cos_b + cos_a * sin_b, cos_a * cos_b - sin_a * sin_b], axis=-1
    )
    waves = waves.reshape(seq_len, width).astype(bf16)

    done = layer(
        float(places * seq_len),
        block,
        dict(inverse=inverse, order=block_order),
        dict(
            tokens=tokens[0],
            teacher=teacher[0],
            mask=valid_mask,
            gain_rows=gain_rows,
            bias_rows=bias_rows,
            neighbours=neighbours.reshape(-1, width),
            waves_any=waves,
            query_any=query_weight,
            key_any=key_weight,
            value_any=value_weight,
            relative_any=relative_weight,
            cross_query_any=cross_query_weight,
            cross_key_any=cross_key_weight,
            cross_value_any=cross_value_weight,
            up_any=up_weight,
            output_any=output_weight,
            cross_out_any=cross_output_weight,
            down_any=down_weight,
        ),
        1,
    )
    pair_slots = jnp.arange(ctx_count)[:, None, None]
    bias_slots = jnp.where(pair_slots == here, done.bias_grad[None, 0:2], 0.0)
    gain_part = done.gain_grad
    small = jnp.concatenate(
        [
            jnp.pad(gain_part[2:3], ((0, 0), (0, attn - width))),
            jnp.pad(gain_part[0:2], ((0, 0), (0, attn - width))),
            bias_slots.reshape(2, attn),
            jnp.broadcast_to(done.error[0:1, 0:1], (3, attn)),
        ],
        axis=0,
    )
    last = finish(
        dict(
            query_grad=done.query_grad_out,
            table_grad=done.table_grad,
            small=small,
            down_share=done.down_share,
            up_share=done.up_share,
            cross_share=done.cross_share,
            ctx_o_half=done.ctx_o_half,
            out_o_half=done.out_o_half,
            one_grad=done.one_grad,
            tokens=tokens[0],
            gains=done.gains,
            normed_a_any=done.normed_a_any,
            waves_any=waves,
            near_any=done.pair_grad_any,
            pair_cols_any=done.pair_cols_any,
            query_any=query_weight,
            key_any=key_weight,
            value_any=value_weight,
        ),
        2,
    )
    total = last.total
    gain_out = lax.dynamic_slice_in_dim(total[0:3], place * share, share, 1)
    bias_out = lax.dynamic_slice_in_dim(total[3:5].reshape(ctx_count, 2, 128), place * 2, 2, 0)
    bias_out = bias_out.transpose(1, 0, 2).reshape(2, cols)
    loss = total[5, 0] / (2.0 * done.count[0, 0] * width)
    pair_out = last.pair_out.astype(f32)
    down_out = last.down_out.reshape(down_weight.shape).astype(f32)
    cross_output_out = last.cross_o_out.reshape(cols, width).astype(f32)
    output_out = last.output_out.reshape(cols, width).astype(f32)

    return (
        done.layer_out[None],
        loss,
        last.tokens_grad[None],
        last.near_grad.reshape(neighbours.shape),
        pair_out[0],
        pair_out[1],
        pair_out[2],
        output_out,
        pair_out[3],
        bias_out[0],
        bias_out[1],
        last.cross_out[0],
        last.cross_out[1],
        last.cross_out[2],
        cross_output_out,
        last.up_out,
        down_out,
        gain_out[0],
        gain_out[1],
        gain_out[2],
    )


def solution(mesh):
    row = P("wa", None)
    flat = P("wa")
    in_specs = (
        P("wa", "ctx", None),
        P("wa", "ctx", None, None),
        P("wa", "ctx", None),
        P("wa", "ctx"),
        P(),
        row,
        row,
        row,
        row,
        row,
        flat,
        flat,
        row,
        row,
        row,
        row,
        row,
        row,
        flat,
        flat,
        flat,
    )
    out_specs = (
        P("wa", "ctx", None),
        P(),
        P("wa", "ctx", None),
        P("wa", "ctx", None, None),
        row,
        row,
        row,
        row,
        row,
        flat,
        flat,
        row,
        row,
        row,
        row,
        row,
        row,
        flat,
        flat,
        flat,
    )
    by_heads = mesh.shape["ctx"] == 8 and mesh.shape["wa"] == 4
    local = local_by_heads if by_heads else local_general
    return jax.shard_map(local, mesh=mesh, in_specs=in_specs, out_specs=out_specs, check_vma=False)
```

profile of v0, /device:TPU:0, one launch (start us, length us, event | category | flops | bytes accessed | tf_op | source)
XLA Modules:
  0.0 361.3 jit_solution(7023601198317328163)
XLA Ops:
  0.7 0.1 rev.7
  0.8 0.5 multiply_cosine_fusion
  1.3 0.1 rev.6
  1.4 0.2 multiply_sine_fusion.1
  1.6 0.7 add_convert_fusion
  2.4 1.8 pad_maximum_fusion.refs_8_.refs_12_
  4.2 0.1 pad.23.clone
  4.3 0.7 maximum_maximum_fusion.refs_5_
  5.0 0.6 pad_maximum_fusion.1.refs_6_
  5.6 0.6 select_reduce_fusion.refs_0_
  6.3 211.2 %layer.1 = (f32[128,896]{1,0:T(8,128)}, f32[8,128]{1,0:T(8,128)}, f32[8,128]{1,0:T(8,128)}, f32[8,896]{1,0:T(8,128)}, bf16[1024,896]{1,0:T(8,128)(2,1)}, /*index...) custom-call(s32[16]{0:T(128)} %select_reduce_fusion.refs_0_, ...), custom_call_target="tpu_custom_call" | custom-call | tf_op jit(solution)/shard_map/layer/pallas_call | solution.py:1416
  217.5 0.7 slice.64
  218.3 0.8 slice.63
  219.0 0.8 slice.62
  219.8 1.2 slice.65
  221.0 0.6 broadcast_in_dim.81
  221.7 0.7 fusion.1.refs_2_
  222.4 118.7 %finish.1 = (f32[128,896]{1,0:T(8,128)}, f32[512,896]{1,0:T(8,128)}, f32[8,1024]{1,0:T(8,128)}, bf16[8,112,896]{2,1,0:T(8,128)(2,1)}, f32[224,3584]{1,0:T(8,128)...) custom-call(bf16[8,128,384]{2,1,0:T(8,128)(2,1)} %get-tuple-element., ...), custom_call_target="tpu_custom_call" | custom-call | tf_op jit(solution)/shard_map/finish/pallas_call | solution.py:1767
  341.1 2.6 bitcast_convert_fusion.1
  343.7 0.4 convert_element_type.26
  344.1 1.4 copy-done.1
  345.5 2.8 slice_bitcast_fusion
  348.3 2.0 bitcast_convert_fusion
  350.4 0.6 fusion.4
  351.0 0.6 fusion.3
  351.6 0.5 slice.66
  352.1 1.2 slice.67
  354.6 0.8 copy.45
  355.4 0.8 copy.46
  356.2 1.2 copy.47
  357.4 0.7 copy-done
  358.1 1.7 copy.48
  (45 shorter events, 0.3 us)
Async XLA Ops:
  2.3 2.0 copy-start.9
  2.3 2.0 copy-start.10
  2.3 2.0 copy-start.11
  2.3 2.7 copy-start.12
  2.3 2.6 copy-start.13
  2.4 3.3 copy-start.8
  341.1 2.7 copy-start.3
  343.7 1.8 copy-start.1
  345.5 2.8 copy-start.4
  348.3 2.0 copy-start.7
  348.3 6.3 %copy-start.5 = (f32[128,896]{1,0:T(8,128)S(1)}, f32[128,896]{1,0:T(8,128)}, u32[]{:S(2)}) copy-start(f32[128,896]{1,0:T(8,128)} %get-tuple-element.46) | copy-start | bytes 1376260
  348.3 7.1 %copy-start.6 = (f32[128,896]{1,0:T(8,128)S(1)}, f32[128,896]{1,0:T(8,128)}, u32[]{:S(2)}) copy-start(f32[128,896]{1,0:T(8,128)} %get-tuple-element.64) | copy-start | bytes 1376260
  350.3 5.8 %copy-start.2 = (f32[512,896]{1,0:T(8,128)S(1)}, f32[512,896]{1,0:T(8,128)}, u32[]{:S(2)}) copy-start(f32[512,896]{1,0:T(8,128)} %get-tuple-element.65) | copy-start | bytes 5505028
  355.4 2.7 copy-start
where the time goes:
time: 369 us; the launch traced here: 361 us
  Pallas kernels  330 us (89%)
  local copies, waits for them, and re-layouts  16.8 us (5%)
  other arithmetic  11 us (3%)
  between operations  3.7 us (1%)
    pallas_call x1, Pallas kernels, layer(): pl.pallas_call(functools.partial(layer_kernel, names, total_tokens, block...  211 us
    pallas_call x1, Pallas kernels, finish(): pl.pallas_call(functools.partial(finish_kernel, names), out_shape=list(re...  119 us

commit v1 on v0

--- a/solution.py
+++ b/solution.py
@@ -996,6 +996,11 @@
     near_sum.start()
     for part in pair:
         part.start()
+    near_load.wait()
+    near_gather.start()
+    for part in cross:
+        part.start()
+    up_columns.start()
     gather.step(0)
     near_sum.finish()
     v.count[...] = jnp.broadcast_to(v.small_all[5:6, 0:128], v.count.shape)
@@ -1003,11 +1008,6 @@
     gather.step(1)
     for part in pair:
         part.finish()
-    near_load.wait()
-    near_gather.start()
-    for part in cross:
-        part.start()
-    up_columns.start()
     for copy in early:
         copy.wait()
     v.table[0:seq_len, :] = dot_nn(v.waves[...], v.pair[:, 384:512]).astype(bf16)
@@ -1029,9 +1029,8 @@
         return carry
 
     lax.fori_loop(0, 8, project, 0)
-    normed_out = pltpu.make_async_copy(v.normed_a, v.normed_a_any, local.take(1).at[0])
-    normed_out.start()
-    pair_out = pltpu.make_async_copy(v.pair_cols, v.pair_cols_any, local.take(1).at[0])
+    leaving = Leaving(v, local)
+    leaving.leave("normed_a")
     for place in range(seq_len // block):
         take_block(v.qkv, v.inverse, place, v.qkv_order.at[place * block : (place + 1) * block, :])
     attend_tiles(v.qkv_order, v.table, v.biases[3:4, :], v.biases[4:5, :], v.heads_order)
@@ -1041,11 +1040,6 @@
         take_block(v.heads_order, v.order, place, v.heads.at[place // per, at : at + block, :])
     out_swap = SwapHeads(v.heads, v.attended, True, send.take(8), recv.take(8))
     out_swap.start_out()
-    near_gather.near()
-    near_gather.relay()
-    for part in cross:
-        part.relay()
-    up_columns.relay()
     for copy in late:
         copy.wait()
 
@@ -1061,6 +1055,11 @@
     sums[0].give_near(output_part(1))
     out_swap.wait_rows(2)
     sums[0].pass_on(output_part(2))
+    near_gather.near()
+    near_gather.relay()
+    for part in cross:
+        part.relay()
+    up_columns.relay()
     out_swap.wait_rows(0)
     v.hidden_one[...] = v.tokens[...].astype(f32) + sums[0].total(output_part(0))
     value = v.hidden_one[...]
@@ -1071,7 +1070,7 @@
     near_gather.far()
     for part in cross:
         part.finish()
-    pair_out.start()
+    leaving.leave("pair_cols")
     near_count = v.near.shape[1]
 
     def near_project(r, carry):
@@ -1093,7 +1092,7 @@
             v.crossed[pl.ds(at, GROUP), :] = join_all(out).astype(bf16)
             return carry
 
-        lax.fori_loop(0, tok // GROUP, group, 0)
+        lax.fori_loop(0, tok // GROUP, group, 0, unroll=True)
         return dot_nn(v.crossed[r * tok : (r + 1) * tok, :], v.cross_out_w[...])
 
     def in_turn(gathered, summed, part, between=None):
@@ -1131,19 +1130,38 @@
     same = lax.broadcasted_iota(jnp.int32, square, 0) == lax.broadcasted_iota(jnp.int32, square, 1)
     valid = jnp.sum(jnp.where(same, mask, 0.0), axis=1, keepdims=True)
     weighted = valid * error
-    v.error[...] = jnp.broadcast_to(jnp.sum(weighted * error, keepdims=True), v.error.shape)
+    v.small[0:5, :] = jnp.zeros((5, 1024), f32)
+    v.small[5:6, :] = jnp.broadcast_to(jnp.sum(weighted * error, keepdims=True), (1, 1024))
+    v.small[6:8, :] = jnp.broadcast_to(v.count[0:1, 0:1], (2, 1024))
     v.out_grad[...] = (total_tokens / v.count[0:1, 0:1]) * weighted
 
-    middle_back(v, send, recv, local, block)
-    normed_out.wait()
-    pair_out.wait()
+    leaving.leave("layer_out")
+    middle_back(v, send, recv, leaving, block)
+    leaving.finish()
+
+
+class Leaving:
+
+    def __init__(self, v, local):
+        self.v, self.local, self.copies = v, local, []
+
+    def leave(self, name):
+        copy = pltpu.make_async_copy(
+            getattr(self.v, name), getattr(self.v, name + "_any"), self.local.take(1).at[0]
+        )
+        copy.start()
+        self.copies.append(copy)
+
+    def finish(self):
+        for copy in self.copies:
+            copy.wait()
 
 
 def take_block(source, chosen, place, target):
     target[...] = source[chosen[place]]
 
 
-def middle_back(v, send, recv, local, block):
+def middle_back(v, send, recv, leaving, block):
     c, w = places_here()
     tok, width = v.tokens.shape
     rows = 4 * tok
@@ -1211,13 +1229,13 @@
             delta = jnp.sum(shares * share_grad, axis=1, keepdims=True)
             score_grad = (shares * (share_grad - delta)).astype(bf16)
             query_grad = join_all(dot_nn(score_grad, keys)) * scale
-            v.query_grad[pl.ds(at, GROUP), :] = query_grad.astype(bf16)
+            v.cross_grad[pl.ds(at, GROUP), :] = query_grad.astype(bf16)
             v.pair_grad[near, 0:cols] = (dot_tn(score_grad, query) * scale).astype(bf16)
             v.pair_grad[near, cols:] = dot_tn(shares.astype(bf16), grad).astype(bf16)
             return carry
 
-        lax.fori_loop(0, tok // GROUP, group, 0)
-        return dot_nt(v.query_grad[part, :], v.query_cols[...])
+        lax.fori_loop(0, tok // GROUP, group, 0, unroll=True)
+        return dot_nt(v.cross_grad[part, :], v.query_cols[...])
 
     v.keep[0] = cross_back(0)
     second.near()
@@ -1229,21 +1247,20 @@
     down.start_z()
     sum_b.give_far(cross_back(3))
     sum_b.pass_on(v.keep[2])
-    pair_grad_out = pltpu.make_async_copy(v.pair_grad, v.pair_grad_any, local.take(1).at[0])
-    pair_grad_out.start()
+    leaving.leave("pair_grad")
     normed_b = v.rows_b[...].reshape(rows, width)
     put_rows(v.cross_out_x, dot_tn(v.crossed[...], v.rows_two[...].reshape(rows, width)))
     ctx_o.start_y()
-    put_shares(v.cross_x, dot_tn(normed_b, v.query_grad[...]), 0)
+    put_shares(v.cross_x, dot_tn(normed_b, v.cross_grad[...]), 0)
     normed_grad = sum_b.total(v.keep[0])
     value = v.hidden_one[...]
     inverse = inverse_rms(value)
     one_grad = v.keep[1] + norm_pull(value, inverse, v.gains[1:2, :], normed_grad)
     gain_two = jnp.sum(normed_grad * value * inverse, axis=0, keepdims=True)
-    v.gain_grad[...] = jnp.concatenate(
-        [gain_two, gain_three, jnp.zeros((6, gain_two.shape[1]), f32)], axis=0
-    )
+    v.small[1:2, 0:width] = gain_two
+    v.small[2:3, 0:width] = gain_three
     v.one_grad[...] = one_grad
+    leaving.leave("one_grad")
     v.rows_one[0] = one_grad.astype(bf16)
 
     third.start()
@@ -1268,6 +1285,9 @@
     put_rows(v.output_x, dot_tn(attended, v.rows_one[...].reshape(rows, width)))
     out_o.start_y()
     heads.finish_in()
+    leaving.leave("gains")
+    cross.finish_y()
+    cross.start_z()
 
     per = tok // block
     for place in range(8 * per):
@@ -1281,14 +1301,16 @@
     def poll(tile):
         if tile == 1:
             down.finish_z()
+            leaving.leave("down_share")
         if tile == 3:
             ctx_o.finish_y()
-            cross.finish_y()
-            cross.start_z()
-        if tile == 5:
+            leaving.leave("ctx_o_half")
+        if tile == 4:
+            up.finish_z()
+            leaving.leave("up_share")
+        if tile == 6:
             out_o.finish_y()
-        if tile == 6:
-            up.finish_z()
+            leaving.leave("out_o_half")
 
     content_sum, position_sum = attend_back_tiles(
         v.qkv_order,
@@ -1303,14 +1325,20 @@
         poll,
     )
     v.table_grad[...] = v.drel[0 : v.table_grad.shape[0], :] * scale
-    v.bias_grad[...] = jnp.concatenate([content_sum, position_sum, jnp.zeros((6, 128), f32)], axis=0)
+    leaving.leave("table_grad")
+    both = jnp.concatenate([content_sum, position_sum] * 4, axis=1)
+    pairs = lax.broadcasted_iota(jnp.int32, both.shape, 1) // 256
+    v.small[3:4, :] = jnp.where(pairs == c, both, 0.0)
+    v.small[4:5, :] = jnp.where(pairs + 4 == c, both, 0.0)
+    leaving.leave("small")
     for place in range(8 * per):
         at = (place % per) * block
         take_block(
-            v.qkv_grad_order, v.order, place, v.query_grad_out.at[place // per, at : at + block, :]
+            v.qkv_grad_order, v.order, place, v.query_grad.at[place // per, at : at + block, :]
         )
+    leaving.leave("query_grad")
     cross.finish_z()
-    pair_grad_out.wait()
+    leaving.leave("cross_share")
 
 
 def layer(total_tokens, block, orders, given, collective_id):
@@ -1325,36 +1353,32 @@
     shape = jax.ShapeDtypeStruct
     vmem = pltpu.VMEM
     dma = pltpu.SemaphoreType.DMA
-    results = dict(
+    kept = dict(
         layer_out=shape((tok, width), f32),
-        error=shape((8, 128), f32),
-        count=shape((8, 128), f32),
+        small=shape((8, 1024), f32),
         gains=shape((8, width), f32),
-        normed_a_any=shape((seq_len, width), bf16),
-        pair_cols_any=shape((width, 2 * cols), bf16),
+        normed_a=shape((seq_len, width), bf16),
+        pair_cols=shape((width, 2 * cols), bf16),
         one_grad=shape((tok, width), f32),
-        gain_grad=shape((8, width), f32),
-        pair_grad_any=shape((4 * near, 2 * cols), bf16),
-        query_grad_out=shape((8, tok, 384), bf16),
+        pair_grad=shape((4 * near, 2 * cols), bf16),
+        query_grad=shape((8, tok, 384), bf16),
         table_grad=shape((seq_len, 128), f32),
-        bias_grad=shape((8, 128), f32),
         down_share=shape((hidden // 8, width), bf16),
         up_share=shape((4, padded, hidden), bf16),
         cross_share=shape((4, padded, 3 * cols), bf16),
         ctx_o_half=shape((4, cols // 8, width), bf16),
         out_o_half=shape((4, cols // 8, width), bf16),
     )
+    results = {name + "_any": value for name, value in kept.items()}
     scratch = dict(
         small_all=vmem((8, 1024), f32),
         small_near=vmem((3, 8, 1024), f32),
         qkv=vmem((seq_len // block, block, 384), bf16),
         table=vmem((seq_len + TILE, 128), bf16),
         biases=vmem((8, 128), f32),
-        normed_a=vmem((seq_len, width), bf16),
-        pair_cols=vmem((width, 2 * cols), bf16),
+        count=vmem((8, 128), f32),
         heads_grad=vmem((8, tok, 128), bf16),
         grad_order=vmem((seq_len, 128), bf16),
-        pair_grad=vmem((4 * near, 2 * cols), bf16),
         qkv_grad_order=vmem((seq_len // block, block, 384), bf16),
         dkey=vmem((seq_len, 128), f32),
         dvalue=vmem((seq_len, 128), f32),
@@ -1396,7 +1420,7 @@
         take=vmem((5, 3, tok, width), bf16),
         keep=vmem((3, tok, width), f32),
         pre_grad=vmem((rows, hidden), bf16),
-        query_grad=vmem((rows, cols), bf16),
+        cross_grad=vmem((rows, cols), bf16),
         heads_out=vmem((4, tok, cols), bf16),
         down_x=vmem((4, 2, hidden // 8, width), bf16),
         down_half=vmem((4, hidden // 8, width), bf16),
@@ -1407,8 +1431,9 @@
         cross_x=vmem((4, 2, 4, padded, 3 * cols), bf16),
         send=dma((232,)),
         recv=dma((232,)),
-        local=dma((8,)),
-    )
+        local=dma((24,)),
+    )
+    scratch.update({name: vmem(value.shape, value.dtype) for name, value in kept.items()})
     names = [*orders, *given, *results, *scratch]
     specs = [in_smem] * len(orders) + [
         any_space if name.endswith("_any") or name == "neighbours" else in_vmem for name in given
@@ -1417,14 +1442,14 @@
         functools.partial(layer_kernel, names, total_tokens, block),
         out_shape=list(results.values()),
         in_specs=specs,
-        out_specs=[any_space if name.endswith("_any") else in_vmem for name in results],
+        out_specs=[any_space] * len(results),
         scratch_shapes=list(scratch.values()),
         compiler_params=pltpu.CompilerParams(
             collective_id=collective_id, has_side_effects=True, vmem_limit_bytes=62 * 2**20
         ),
         name="layer",
     )(*orders.values(), *given.values())
-    return types.SimpleNamespace(**dict(zip(results, got, strict=True)))
+    return types.SimpleNamespace(**dict(zip(kept, got, strict=True)))
 
 
 class Spread:
@@ -1541,6 +1566,7 @@
 
     loads = [load(v.normed_a_any, v.normed_a), load(v.waves_any, v.waves)]
     late = [load(v.pair_cols_any, v.pair_cols), load(v.near_any, v.near_rows)]
+    leaving = Leaving(v, local)
 
     def line(out):
         return LineGather(out, send.take(13), recv.take(13))
@@ -1673,6 +1699,7 @@
     hidden = v.tokens[...].astype(f32)
     inverse = inverse_rms(hidden)
     v.tokens_grad[...] = v.one_grad[...] + norm_pull(hidden, inverse, v.gains[0:1, :], normed_grad)
+    leaving.leave("tokens_grad")
     v.total[...] = v.small[...]
     v.total[0:1, 0:width] = jnp.sum(normed_grad * hidden * inverse, axis=0, keepdims=True)
     stages[0].start()
@@ -1681,37 +1708,46 @@
     stages[0].finish()
     stages[1].start()
     v.near_grad[...] = sum_near.total(v.near_grad[...])
+    leaving.leave("near_grad")
     stages[1].finish()
     stages[2].start()
     down.finish()
+    leaving.leave("down_out")
     up.finish()
     used = share // 8
-
-    def lay_up(part, at):
-        v.up_out[at : at + used, :] = v.up_all[part, 0:used, :].astype(f32)
-
     for part in range(8):
-        lay_up(part, part * used)
+        v.up_out[part * used : (part + 1) * used, :] = v.up_all[part, 0:used, :].astype(f32)
+    leaving.leave("up_out")
     pair.finish()
+    pair_outs = (v.query_out, v.key_out, v.value_out, v.relative_out)
     for part in range(8):
-        for m in range(4):
-            v.pair_out[m, :, 128 * part : 128 * (part + 1)] = v.pair_all[
-                part, :, 128 * m : 128 * (m + 1)
-            ]
+        for m, out in enumerate(pair_outs):
+            out[:, 128 * part : 128 * (part + 1)] = v.pair_all[part, :, 128 * m : 128 * (m + 1)]
+    for name in ("query_out", "key_out", "value_out", "relative_out"):
+        leaving.leave(name)
     ctx_o.finish()
+    leaving.leave("cross_o_out")
     out_o.finish()
+    leaving.leave("output_out")
     cross.finish()
-    for part in range(8):
-        for m in range(3):
+    for m, out in enumerate((v.cross_query_out, v.cross_key_out, v.cross_value_out)):
+        for part in range(8):
             for place in range(4):
                 at = (place * 3 + m) * cols
-                v.cross_out[m, part * used : (part + 1) * used, place * cols : (place + 1) * cols] = (
-                    v.cross_all[part, 0:used, at : at + cols].astype(f32)
-                )
+                out[part * used : (part + 1) * used, place * cols : (place + 1) * cols] = v.cross_all[
+                    part, 0:used, at : at + cols
+                ].astype(f32)
+    for name in ("cross_query_out", "cross_key_out", "cross_value_out"):
+        leaving.leave(name)
     stages[2].finish()
+    devices = 32.0
+    loss = v.total[5:6, :] * devices / (2.0 * width * v.total[6:7, :])
+    v.total[7:8, :] = loss
+    leaving.leave("total")
     for j in range(1, 8):
         for m in range(3):
             block_copy(j, m, c).wait_send()
+    leaving.finish()
 
 
 def finish(given, collective_id):
@@ -1726,17 +1762,23 @@
     vmem = pltpu.VMEM
     dma = pltpu.SemaphoreType.DMA
     part = (cols // 8, width)
-    results = dict(
+    kept = dict(
         tokens_grad=shape((tok, width), f32),
         near_grad=shape((near // 4, width), f32),
         total=shape(given["small"].shape, f32),
         down_out=shape((8,) + given["down_share"].shape, bf16),
         up_out=shape((share, 4 * hidden), f32),
-        cross_out=shape((3, share, 4 * cols), f32),
+        cross_query_out=shape((share, 4 * cols), f32),
+        cross_key_out=shape((share, 4 * cols), f32),
+        cross_value_out=shape((share, 4 * cols), f32),
         cross_o_out=shape((8,) + part, bf16),
         output_out=shape((8,) + part, bf16),
-        pair_out=shape((4, share, 1024), bf16),
-    )
+        query_out=shape((share, 1024), bf16),
+        key_out=shape((share, 1024), bf16),
+        value_out=shape((share, 1024), bf16),
+        relative_out=shape((share, 1024), bf16),
+    )
+    results = {name + "_any": value for name, value in kept.items()}
     scratch = dict(
         normed_a=vmem(given["normed_a_any"].shape, bf16),
         waves=vmem(given["waves_any"].shape, bf16),
@@ -1761,21 +1803,22 @@
         got_z=vmem((3,) + given["small"].shape, f32),
         send=dma((184,)),
         recv=dma((184,)),
-        local=dma((4,)),
-    )
+        local=dma((24,)),
+    )
+    scratch.update({name: vmem(value.shape, value.dtype) for name, value in kept.items()})
     names = [*given, *results, *scratch]
     got = pl.pallas_call(
         functools.partial(finish_kernel, names),
         out_shape=list(results.values()),
         in_specs=[any_space if name.endswith("_any") else in_vmem for name in given],
-        out_specs=[in_vmem] * len(results),
+        out_specs=[any_space] * len(results),
         scratch_shapes=list(scratch.values()),
         compiler_params=pltpu.CompilerParams(
             collective_id=collective_id, has_side_effects=True, vmem_limit_bytes=62 * 2**20
         ),
         name="finish",
     )(*given.values())
-    return types.SimpleNamespace(**dict(zip(results, got, strict=True)))
+    return types.SimpleNamespace(**dict(zip(kept, got, strict=True)))
 
 
 def skew(wide, count):
@@ -2255,23 +2298,11 @@
         ),
         1,
     )
-    pair_slots = jnp.arange(ctx_count)[:, None, None]
-    bias_slots = jnp.where(pair_slots == here, done.bias_grad[None, 0:2], 0.0)
-    gain_part = done.gain_grad
-    small = jnp.concatenate(
-        [
-            jnp.pad(gain_part[2:3], ((0, 0), (0, attn - width))),
-            jnp.pad(gain_part[0:2], ((0, 0), (0, attn - width))),
-            bias_slots.reshape(2, attn),
-            jnp.broadcast_to(done.error[0:1, 0:1], (3, attn)),
-        ],
-        axis=0,
-    )
     last = finish(
         dict(
-            query_grad=done.query_grad_out,
+            query_grad=done.query_grad,
             table_grad=done.table_grad,
-            small=small,
+            small=done.small,
             down_share=done.down_share,
             up_share=done.up_share,
             cross_share=done.cross_share,
@@ -2280,10 +2311,10 @@
             one_grad=done.one_grad,
             tokens=tokens[0],
             gains=done.gains,
-            normed_a_any=done.normed_a_any,
+            normed_a_any=done.normed_a,
             waves_any=waves,
-            near_any=done.pair_grad_any,
-            pair_cols_any=done.pair_cols_any,
+            near_any=done.pair_grad,
+            pair_cols_any=done.pair_cols,
             query_any=query_weight,
             key_any=key_weight,
             value_any=value_weight,
@@ -2294,8 +2325,7 @@
     gain_out = lax.dynamic_slice_in_dim(total[0:3], place * share, share, 1)
     bias_out = lax.dynamic_slice_in_dim(total[3:5].reshape(ctx_count, 2, 128), place * 2, 2, 0)
     bias_out = bias_out.transpose(1, 0, 2).reshape(2, cols)
-    loss = total[5, 0] / (2.0 * done.count[0, 0] * width)
-    pair_out = last.pair_out.astype(f32)
+    loss = total[7, 0]
     down_out = last.down_out.reshape(down_weight.shape).astype(f32)
     cross_output_out = last.cross_o_out.reshape(cols, width).astype(f32)
     output_out = last.output_out.reshape(cols, width).astype(f32)
@@ -2305,16 +2335,16 @@
         loss,
         last.tokens_grad[None],
         last.near_grad.reshape(neighbours.shape),
-        pair_out[0],
-        pair_out[1],
-        pair_out[2],
+        last.query_out.astype(f32),
+        last.key_out.astype(f32),
+        last.value_out.astype(f32),
         output_out,
-        pair_out[3],
+        last.relative_out.astype(f32),
         bias_out[0],
         bias_out[1],
-        last.cross_out[0],
-        last.cross_out[1],
-        last.cross_out[2],
+        last.cross_query_out,
+        last.cross_key_out,
+        last.cross_value_out,
         cross_output_out,
         last.up_out,
         down_out,

time: 369 us -> 355 us (0.962)
  Pallas kernels: 330 us -> 317 us
  other arithmetic: 11 us -> 15.4 us
    pallas_call x1, Pallas kernels: 211 us -> 201 us  [layer(): pl.pallas_call(functools.partial(layer_kernel, names, total_tokens, block...]
    convert_element_type x1 -> x4, other arithmetic: 0.41 us -> 6.12 us  [the longest x1 2.04 us: local_by_heads(): last.query_out.astype(f32)]
    slice x6 -> x1, local copies, waits for them, and re-layouts: 5.07 us -> 1.29 us  [local_by_heads(): loss = total[7, 0]]
    unnamed x32 -> x33, local copies, waits for them, and re-layouts: 6.61 us -> 8.05 us
where the time goes in v1:
time: 355 us; the launch traced here: 348 us
  Pallas kernels  317 us (89%)
  other arithmetic  15.4 us (4%)
  local copies, waits for them, and re-layouts  14.2 us (4%)
    pallas_call x1, Pallas kernels, layer(): pl.pallas_call(functools.partial(layer_kernel, names, total_tokens, block...  201 us
    pallas_call x1, Pallas kernels, finish(): pl.pallas_call(functools.partial(finish_kernel, names), out_shape=list(re...  116 us
    unnamed x33, local copies, waits for them, and re-layouts  8.05 us

profile of v1, /device:TPU:0, one launch (start us, length us, event | category | flops | bytes accessed | tf_op | source)
XLA Modules:
  0.0 347.9 jit_solution(2827578555296463256)
XLA Ops:
  0.7 1.3 select_reduce_fusion.refs_0_
  1.9 0.7 stack.11
  2.6 0.7 stack.10
  3.3 0.7 stack.9
  4.0 0.7 maximum_maximum_fusion.refs_5_
  4.7 0.7 broadcast_in_dim.46
  5.3 0.7 broadcast_in_dim.45
  6.0 0.6 pad_maximum_fusion.1.refs_6_
  6.6 0.1 rev.7
  6.7 0.5 multiply_cosine_fusion
  7.4 0.2 multiply_sine_fusion.1
  7.6 0.7 add_convert_fusion
  8.2 1.8 pad_maximum_fusion.refs_8_.refs_12_
  10.1 201.2 %layer.1 = (f32[128,896]{1,0:T(8,128)}, f32[8,1024]{1,0:T(8,128)}, f32[8,896]{1,0:T(8,128)}, bf16[1024,896]{1,0:T(8,128)(2,1)}, bf16[896,512]{1,0:T(8,128)(2,1)}...) custom-call(s32[16]{0:T(128)} %select_reduce_fusion.refs_0_, ...), custom_call_target="tpu_custom_call" | custom-call | tf_op jit(solution)/shard_map/layer/pallas_call | solution.py:1441
  211.2 116.0 %finish.1 = (f32[128,896]{1,0:T(8,128)}, f32[512,896]{1,0:T(8,128)}, f32[8,1024]{1,0:T(8,128)}, bf16[8,112,896]{2,1,0:T(8,128)(2,1)}, f32[224,3584]{1,0:T(8,128)...) custom-call(bf16[8,128,384]{2,1,0:T(8,128)(2,1)} %get-tuple-element., ...), custom_call_target="tpu_custom_call" | custom-call | tf_op jit(solution)/shard_map/finish/pallas_call | solution.py:1810
  327.3 1.3 slice.26
  328.6 2.0 convert_element_type.31
  330.6 2.0 convert_element_type.32
  332.7 1.0 convert_element_type.33
  333.7 1.4 bitcast_convert_fusion.1
  335.1 1.0 convert_element_type.36
  336.2 0.6 fusion.1
  336.8 2.0 bitcast_convert_fusion
  338.8 0.6 fusion
  339.5 0.8 copy.48
  340.2 0.8 copy.49
  341.0 1.2 copy.50
  342.2 0.9 copy.51
  343.2 0.9 copy.52
  344.1 0.9 copy.53
  345.0 0.8 copy-done
  345.8 1.7 copy.54
  (37 shorter events, 0.3 us)
Async XLA Ops:
  327.3 5.4 %copy-start.11 = (bf16[224,1024]{1,0:T(8,128)(2,1)S(1)}, bf16[224,1024]{1,0:T(8,128)(2,1)}, u32[]{:S(2)}) copy-start(bf16[224,1024]{1,0:T(8,128)(2,1)} %get-tuple-element.67) | copy-start | bytes 1376260
  327.3 6.4 %copy-start.9 = (bf16[8,32,896]{2,1,0:T(8,128)(2,1)S(1)}, bf16[8,32,896]{2,1,0:T(8,128)(2,1)}, u32[]{:S(2)}) copy-start(bf16[8,32,896]{2,1,0:T(8,128)(2,1)} %get-tuple-element.73) | copy-start | bytes 1376260
  327.3 6.4 %copy-start.10 = (bf16[8,32,896]{2,1,0:T(8,128)(2,1)S(1)}, bf16[8,32,896]{2,1,0:T(8,128)(2,1)}, u32[]{:S(2)}) copy-start(bf16[8,32,896]{2,1,0:T(8,128)(2,1)} %get-tuple-element.68) | copy-start | bytes 1376260
  332.7 2.5 copy-start.8
  333.7 2.5 copy-start.12
  333.7 3.1 copy-start.2
  336.8 2.7 copy-start.6
  336.8 3.4 copy-start.7
  338.8 2.2 copy-start.1
  340.2 2.0 copy-start.5
  341.0 2.2 copy-start.4
  342.2 1.9 copy-start.3
  343.2 2.6 copy-start

commit v2 on v1

--- a/solution.py
+++ b/solution.py
@@ -781,6 +781,10 @@
             self.w ^ j,
         )
 
+    def handed(self, place):
+        ref = self.put(place)
+        return remote(ref, ref, self.send.at[3], self.recv.at[3], self.c, self.w ^ 1)
+
     def passed(self, j, half):
         ref = self.put(self.w ^ j, half)
         return remote(ref, ref, self.send.at[2 + j], self.recv.at[2 + j], self.c ^ 1, self.w)
@@ -789,11 +793,16 @@
         return pltpu.make_async_copy(self.taken(self.w), self.put(self.w), self.send.at[0])
 
     def start(self):
-        for j in (2, 3, 1):
+        for j in (2, 3, 1) if self.shared else (2, 1):
             self.copy(j, self.w).start()
         self.own().start()
 
     def relay(self):
+        if not self.shared:
+            self.copy(2, self.w).wait_send()
+            self.copy(2, self.w ^ 2).wait_recv()
+            self.handed(self.w ^ 2).start()
+            return
         for j in (2, 3):
             self.copy(j, self.w).wait_send()
             self.copy(j, self.w ^ j).wait_recv()
@@ -801,10 +810,12 @@
 
     def finish(self):
         self.own().wait()
-        for j in (1,) if self.shared else (1, 2, 3):
-            self.copy(j, self.w).wait_send()
-            self.copy(j, self.w ^ j).wait_recv()
-        if self.shared:
+        self.copy(1, self.w).wait_send()
+        self.copy(1, self.w ^ 1).wait_recv()
+        if not self.shared:
+            self.handed(self.w ^ 2).wait_send()
+            self.handed(self.w ^ 3).wait_recv()
+        else:
             for j in (2, 3):
                 self.passed(j, self.y).wait_send()
                 self.passed(j, 1 - self.y).wait_recv()
@@ -955,22 +966,12 @@
         return copy
 
     near_load = load(v.neighbours, v.near.at[0])
-    early = [load(v.waves_any, v.waves)]
     late = [
         load(v.output_any, v.output_w),
         load(v.cross_out_any, v.cross_out_w),
         load(v.down_any, v.down_w),
     ]
-    column = lax.broadcasted_iota(jnp.int32, (256, 1024), 1)
-    line = lax.broadcasted_iota(jnp.int32, (256, 1024), 0)
-
-    def placed(value, start):
-        chosen = jnp.where(column == line + start, 1.0, 0.0).astype(bf16)
-        return dot_nn(value, chosen[: value.shape[1]])
-
-    v.small_all[...] = placed(v.gain_rows[...], w * (width // 4)) + placed(v.bias_rows[...], w * cols)
     mask = v.mask[...].astype(f32)
-    v.small_all[5:6, :] = jnp.broadcast_to(jnp.sum(mask, keepdims=True), (1, 1024))
     v.tokens_all[c] = v.tokens[...]
     meet_all()
 
@@ -993,23 +994,55 @@
     near_send, near_recv = send.take(3), recv.take(3)
     near_gather = GatherRows(v.near, near_send, near_recv)
     gather.start()
-    near_sum.start()
     for part in pair:
         part.start()
+
+    part_width = width // 4
+    count = 3 * part_width + 2 * cols
+    entry = lax.broadcasted_iota(jnp.int32, (count, 1024), 0)
+    for k in range(1, 3):
+        entry = jnp.where(
+            lax.broadcasted_iota(jnp.int32, (count, 1024), 0) >= k * part_width, entry - part_width, entry
+        )
+    bias = lax.broadcasted_iota(jnp.int32, (count, 1024), 0) - 3 * part_width
+    entry = jnp.where(bias >= 0, bias, entry)
+    entry = jnp.where(bias >= cols, bias - cols, entry)
+    start = jnp.where(bias >= 0, w * cols, w * part_width)
+    chosen = lax.broadcasted_iota(jnp.int32, (count, 1024), 1) == entry + start
+    lane = lax.broadcasted_iota(jnp.int32, (8, count), 1)
+    row = lax.broadcasted_iota(jnp.int32, (8, count), 0)
+    bounds = (0, part_width, 2 * part_width, 3 * part_width, 3 * part_width + cols, count)
+    picked = jnp.zeros((8, count), f32)
+    for k in range(5):
+        inside = (row == k) & (lane >= bounds[k]) & (lane < bounds[k + 1])
+        picked = jnp.where(inside, v.gain_row[...].astype(f32), picked)
+    v.small_all[...] = dot_nn(picked.astype(bf16), jnp.where(chosen, 1.0, 0.0).astype(bf16))
+    v.small_all[5:6, :] = jnp.broadcast_to(jnp.sum(mask, keepdims=True), (1, 1024))
+    near_sum.start()
     near_load.wait()
     near_gather.start()
     for part in cross:
         part.start()
-    up_columns.start()
+
+    def wave_rows(part, carry):
+        start = pl.multiple_of(part * 64, 64)
+        first = v.tables[pl.ds(part, 1), :] * v.tables[32:96, :]
+        second = v.tables[pl.ds(part + 16, 1), :] * v.tables[96:160, :]
+        v.waves[pl.ds(start, 64), :] = (first + second).astype(bf16)
+        return carry
+
+    lax.fori_loop(0, seq_len // 64, wave_rows, 0)
+    leaving = Leaving(v, local)
+    leaving.leave("waves")
     gather.step(0)
     near_sum.finish()
     v.count[...] = jnp.broadcast_to(v.small_all[5:6, 0:128], v.count.shape)
     count_sum.start()
+    for part in pair:
+        part.relay()
     gather.step(1)
     for part in pair:
         part.finish()
-    for copy in early:
-        copy.wait()
     v.table[0:seq_len, :] = dot_nn(v.waves[...], v.pair[:, 384:512]).astype(bf16)
     v.table[seq_len:, :] = jnp.zeros((TILE, 128), bf16)
     v.biases[...] = v.small_all[:, pl.ds(pl.multiple_of(c * 128, 128), 128)]
@@ -1029,7 +1062,6 @@
         return carry
 
     lax.fori_loop(0, 8, project, 0)
-    leaving = Leaving(v, local)
     leaving.leave("normed_a")
     for place in range(seq_len // block):
         take_block(v.qkv, v.inverse, place, v.qkv_order.at[place * block : (place + 1) * block, :])
@@ -1059,7 +1091,6 @@
     near_gather.relay()
     for part in cross:
         part.relay()
-    up_columns.relay()
     out_swap.wait_rows(0)
     v.hidden_one[...] = v.tokens[...].astype(f32) + sums[0].total(output_part(0))
     value = v.hidden_one[...]
@@ -1095,11 +1126,13 @@
         lax.fori_loop(0, tok // GROUP, group, 0, unroll=True)
         return dot_nn(v.crossed[r * tok : (r + 1) * tok, :], v.cross_out_w[...])
 
-    def in_turn(gathered, summed, part, between=None):
+    def in_turn(gathered, summed, part, arrived=None, between=None):
         v.keep[0] = part(0)
         gathered.near()
         summed.give_near(part(1))
         gathered.relay()
+        if arrived is not None:
+            arrived()
         v.keep[2] = part(2)
         gathered.far()
         summed.give_far(part(3))
@@ -1108,7 +1141,9 @@
             between()
         return summed.total(v.keep[0])
 
-    v.hidden_two[...] = v.hidden_one[...] + in_turn(gathers[0], sums[1], cross_part)
+    v.hidden_two[...] = v.hidden_one[...] + in_turn(
+        gathers[0], sums[1], cross_part, up_columns.start, up_columns.relay
+    )
     value = v.hidden_two[...]
     v.rows_c[0] = (value * inverse_rms(value) * gain_three).astype(bf16)
 
@@ -1175,9 +1210,7 @@
     )
     down = CtxSum(send.take(12), recv.take(12), v.down_x, v.down_half, v.down_part, v.down_share)
     up = CtxSum(send.take(12), recv.take(12), v.up_x, v.up_half, v.up_part, v.up_share)
-    cross = CtxSum(
-        send.take(12), recv.take(12), v.cross_x, v.cross_half, v.cross_part, v.cross_share
-    )
+    cross = CtxSum(send.take(12), recv.take(12), v.cross_x, v.cross_half)
     ctx_o = CtxSum(send.take(12), recv.take(12), v.cross_out_x, v.ctx_o_half)
     out_o = CtxSum(send.take(12), recv.take(12), v.output_x, v.out_o_half)
     heads = SwapHeads(v.heads_grad, v.heads_out, False, send.take(8), recv.take(8))
@@ -1266,7 +1299,6 @@
     third.start()
     near = v.near[...].reshape(-1, width)
     put_shares(v.cross_x, dot_tn(near, v.pair_grad[...]), cols)
-    cross.start_y()
 
     def head_back(r):
         v.heads_out[r] = dot_nt(v.rows_one[r], v.output_w[...]).astype(bf16)
@@ -1279,15 +1311,14 @@
     head_back(2)
     third.far()
     head_back(3)
+    attended = jnp.concatenate([v.attended[r] for r in range(4)], axis=0)
+    put_rows(v.output_x, dot_tn(attended, v.rows_one[...].reshape(rows, width)))
+    heads.finish_in()
     up.finish_y()
     up.start_z()
-    attended = jnp.concatenate([v.attended[r] for r in range(4)], axis=0)
-    put_rows(v.output_x, dot_tn(attended, v.rows_one[...].reshape(rows, width)))
+    cross.start_y()
     out_o.start_y()
-    heads.finish_in()
     leaving.leave("gains")
-    cross.finish_y()
-    cross.start_z()
 
     per = tok // block
     for place in range(8 * per):
@@ -1305,12 +1336,6 @@
         if tile == 3:
             ctx_o.finish_y()
             leaving.leave("ctx_o_half")
-        if tile == 4:
-            up.finish_z()
-            leaving.leave("up_share")
-        if tile == 6:
-            out_o.finish_y()
-            leaving.leave("out_o_half")
 
     content_sum, position_sum = attend_back_tiles(
         v.qkv_order,
@@ -1337,8 +1362,12 @@
             v.qkv_grad_order, v.order, place, v.query_grad.at[place // per, at : at + block, :]
         )
     leaving.leave("query_grad")
-    cross.finish_z()
-    leaving.leave("cross_share")
+    cross.finish_y()
+    leaving.leave("cross_half")
+    out_o.finish_y()
+    leaving.leave("out_o_half")
+    up.finish_z()
+    leaving.leave("up_share")
 
 
 def layer(total_tokens, block, orders, given, collective_id):
@@ -1357,6 +1386,7 @@
         layer_out=shape((tok, width), f32),
         small=shape((8, 1024), f32),
         gains=shape((8, width), f32),
+        waves=shape((seq_len, width), bf16),
         normed_a=shape((seq_len, width), bf16),
         pair_cols=shape((width, 2 * cols), bf16),
         one_grad=shape((tok, width), f32),
@@ -1365,7 +1395,7 @@
         table_grad=shape((seq_len, 128), f32),
         down_share=shape((hidden // 8, width), bf16),
         up_share=shape((4, padded, hidden), bf16),
-        cross_share=shape((4, padded, 3 * cols), bf16),
+        cross_half=shape((4, 4, padded, 3 * cols), bf16),
         ctx_o_half=shape((4, cols // 8, width), bf16),
         out_o_half=shape((4, cols // 8, width), bf16),
     )
@@ -1383,14 +1413,11 @@
         dkey=vmem((seq_len, 128), f32),
         dvalue=vmem((seq_len, 128), f32),
         drel=vmem((seq_len + TILE, 128), f32),
-        cross_half=vmem((4, 4, padded, 3 * cols), bf16),
-        cross_part=vmem((3, 4, padded, 3 * cols), bf16),
         cross_out_x=vmem((4, 2, cols // 8, width), bf16),
         output_x=vmem((4, 2, cols // 8, width), bf16),
         count_far=vmem((7, 8, 128), f32),
         tokens_all=vmem((8, tok, width), bf16),
         pair=vmem((width, 512), bf16),
-        waves=vmem((seq_len, width), bf16),
         qkv_order=vmem((seq_len, 384), bf16),
         heads_order=vmem((seq_len // block, block, 128), bf16),
         heads_stored=vmem((seq_len // block, block, 128), bf16),
@@ -1578,6 +1605,7 @@
         line(out)
         for out in (v.down_out, v.up_all, v.cross_all, v.cross_o_out, v.output_out, v.pair_all)
     )
+    cross_sum = summed(None, v.cross_half, v.cross_part, v.cross_share)
     ctx_o_sum = summed(None, v.ctx_o_half, v.ctx_o_part, v.ctx_o_share)
     out_o_sum = summed(None, v.out_o_half, v.out_o_part, v.out_o_share)
     up_spread = Spread(v.up_share, v.up_all, send.take(4), recv.take(4))
@@ -1619,7 +1647,7 @@
     v.down_out[c] = v.down_share[...]
     meet_lines()
     up_spread.start()
-    cross_spread.start()
+    cross_sum.start_z()
     down.start()
     ctx_o_sum.start_z()
     out_o_sum.start_z()
@@ -1640,13 +1668,8 @@
     sum_pair.give_near(v.sums[w ^ 1])
     up_spread.finish()
     up.start()
-    cross_spread.finish()
-    cross.start()
     sum_pair.pass_on(v.sums[w ^ 2])
     down.step(0)
-    for j in (4, 6, 5, 7, 2, 3, 1):
-        for m in range(3):
-            block_copy(j, m, c).start()
     v.pair_all[c] = sum_pair.total(v.sums[w]).astype(bf16)
     pair.start()
     for copy in late:
@@ -1658,13 +1681,19 @@
 
     sum_near.give_far(near_part(3))
     sum_near.give_near(near_part(1))
+    cross_sum.finish_z()
+    cross_spread.start()
     sum_near.pass_on(near_part(2))
-    for weight in weights:
-        weight.start()
     v.near_grad[...] = near_part(0)
     up.step(0)
     down.step(1)
-    cross.step(0)
+    cross_spread.finish()
+    cross.start()
+    for j in (4, 6, 5, 7, 2, 3, 1):
+        for m in range(3):
+            block_copy(j, m, c).start()
+    for weight in weights:
+        weight.start()
     ctx_o_sum.finish_z()
     v.cross_o_out[c] = v.ctx_o_share[...]
     ctx_o.start()
@@ -1672,13 +1701,13 @@
     v.output_out[c] = v.out_o_share[...]
     out_o.start()
     up.step(1)
-    cross.step(1)
+    cross.step(0)
     pair.step(0)
     down.step(2)
     ctx_o.step(0)
     out_o.step(0)
     up.step(2)
-    cross.step(2)
+    cross.step(1)
     pair.step(1)
     ctx_o.step(1)
     out_o.step(1)
@@ -1705,6 +1734,7 @@
     stages[0].start()
     ctx_o.step(2)
     out_o.step(2)
+    cross.step(2)
     stages[0].finish()
     stages[1].start()
     v.near_grad[...] = sum_near.total(v.near_grad[...])
@@ -1790,6 +1820,8 @@
         up_all=vmem((8, padded, 4 * hidden), bf16),
         cross_all=vmem((8, padded, 12 * cols), bf16),
         pair_all=vmem((8, share, 512), bf16),
+        cross_part=vmem((3, 4, padded, 3 * cols), bf16),
+        cross_share=vmem((4, padded, 3 * cols), bf16),
         ctx_o_part=vmem((3,) + part, bf16),
         ctx_o_share=vmem(part, bf16),
         out_o_part=vmem((3,) + part, bf16),
@@ -2255,22 +2287,14 @@
     slots = jnp.arange(2 * ctx_count)
     inverse = jnp.sum(jnp.where(block_order[None, :] == slots[:, None], slots[None, :], 0), axis=1)
     inverse = inverse.astype(jnp.int32)
-    gain_rows = jnp.concatenate(
-        [jnp.stack([attention_gain, cross_gain, feedforward_gain]), jnp.zeros((5, share), bf16)]
-    )
-    blank = jnp.zeros((3, cols), bf16)
-    bias_rows = jnp.concatenate([blank, content_bias[None], position_bias[None], blank])
-
     half = width // 2
     freq = jnp.exp(-jnp.log(10000.0) * jnp.arange(half, dtype=f32) * 2.0 / width)
     coarse = (64.0 * jnp.arange(seq_len // 64, dtype=f32)[::-1])[:, None] * freq
     fine = jnp.arange(64, dtype=f32)[::-1][:, None] * freq
-    sin_a, cos_a = jnp.sin(coarse)[:, None], jnp.cos(coarse)[:, None]
-    sin_b, cos_b = jnp.sin(fine)[None], jnp.cos(fine)[None]
-    waves = jnp.concatenate(
-        [sin_a * cos_b + cos_a * sin_b, cos_a * cos_b - sin_a * sin_b], axis=-1
-    )
-    waves = waves.reshape(seq_len, width).astype(bf16)
+    sin_a, cos_a, sin_b, cos_b = jnp.sin(coarse), jnp.cos(coarse), jnp.sin(fine), jnp.cos(fine)
+    left = jnp.concatenate([sin_a, cos_a, cos_b, sin_b], axis=0)
+    right = jnp.concatenate([cos_a, -sin_a, cos_b, sin_b], axis=0)
+    tables = jnp.concatenate([left, right], axis=1)
 
     done = layer(
         float(places * seq_len),
@@ -2280,10 +2304,11 @@
             tokens=tokens[0],
             teacher=teacher[0],
             mask=valid_mask,
-            gain_rows=gain_rows,
-            bias_rows=bias_rows,
+            gain_row=jnp.concatenate(
+                [attention_gain, cross_gain, feedforward_gain, content_bias, position_bias]
+            )[None],
+            tables=tables,
             neighbours=neighbours.reshape(-1, width),
-            waves_any=waves,
             query_any=query_weight,
             key_any=key_weight,
             value_any=value_weight,
@@ -2305,14 +2330,14 @@
             small=done.small,
             down_share=done.down_share,
             up_share=done.up_share,
-            cross_share=done.cross_share,
+            cross_half=done.cross_half,
             ctx_o_half=done.ctx_o_half,
             out_o_half=done.out_o_half,
             one_grad=done.one_grad,
             tokens=tokens[0],
             gains=done.gains,
             normed_a_any=done.normed_a,
-            waves_any=waves,
+            waves_any=done.waves,
             near_any=done.pair_grad,
             pair_cols_any=done.pair_cols,
             query_any=query_weight,

time: 355 us -> 344 us (0.969)
  Pallas kernels: 317 us -> 308 us
    pallas_call x1, Pallas kernels: 201 us -> 182 us  [layer(): pl.pallas_call(functools.partial(layer_kernel, names, total_tokens, block...]
    pallas_call x1, Pallas kernels: 116 us -> 125 us  [finish(): pl.pallas_call(functools.partial(finish_kernel, names), out_shape=list(re...]
where the time goes in v2:
time: 344 us; the launch traced here: 337 us
  Pallas kernels  308 us (90%)
  local copies, waits for them, and re-layouts  15.9 us (5%)
  other arithmetic  12.7 us (4%)
    pallas_call x1, Pallas kernels, layer(): pl.pallas_call(functools.partial(layer_kernel, names, total_tokens, block...  182 us
    pallas_call x1, Pallas kernels, finish(): pl.pallas_call(functools.partial(finish_kernel, names), out_shape=list(re...  125 us
    unnamed x33, local copies, waits for them, and re-layouts  9.22 us

profile of v2, /device:TPU:0, one launch (start us, length us, event | category | flops | bytes accessed | tf_op | source)
XLA Modules:
  0.0 337.4 jit_solution(13266543300080110731)
XLA Ops:
  0.7 1.3 select_reduce_fusion.refs_0_
  1.9 3.4 %concatenate.12 = bf16[1184]{0:T(1024)(128)(2,1)S(1)} concatenate(bf16[224]{0:T(256)(128)(2,1)} %param.39, bf16[224]{0:T(256)(128)(2,1)} %param.40, bf16[224]{0:T(256)(128)(2,1)} %param.41, bf16[256]{0:T(256)(128)(2,1)} %param.31, bf16[256]{0:T(256)(128)(2,1)} %param.32), dimensions={0} | concatenate | bytes 4736 | tf_op jit(solution)/shard_map/concatenate | solution.py:2307
  5.4 0.6 broadcast_in_dim.30.refs_5_
  6.0 0.1 rev.7
  6.1 0.5 multiply_cosine_fusion
  6.6 0.1 rev.6
  6.7 0.2 multiply_sine_fusion.1
  6.9 1.0 maximum_maximum_fusion.refs_6_
  7.9 182.4 %layer.1 = (f32[128,896]{1,0:T(8,128)}, f32[8,1024]{1,0:T(8,128)}, f32[8,896]{1,0:T(8,128)}, bf16[1024,896]{1,0:T(8,128)(2,1)}, bf16[1024,896]{1,0:T(8,128)(2,1)...) custom-call(s32[16]{0:T(128)} %select_reduce_fusion.refs_0_, ...), custom_call_target="tpu_custom_call" | custom-call | tf_op jit(solution)/shard_map/layer/pallas_call | solution.py:1468
  190.3 125.2 %finish.1 = (f32[128,896]{1,0:T(8,128)}, f32[512,896]{1,0:T(8,128)}, f32[8,1024]{1,0:T(8,128)}, bf16[8,112,896]{2,1,0:T(8,128)(2,1)}, f32[224,3584]{1,0:T(8,128)...) custom-call(bf16[8,128,384]{2,1,0:T(8,128)(2,1)} %get-tuple-element., ...), custom_call_target="tpu_custom_call" | custom-call | tf_op jit(solution)/shard_map/finish/pallas_call | solution.py:1842
  315.6 0.0 copy-start.11
  315.6 1.2 slice.26
  316.9 2.1 convert_element_type.30
  319.0 2.0 convert_element_type.31
  321.0 0.0 copy-done.11
  321.0 1.0 convert_element_type.32
  322.0 0.0 copy-done.10
  322.1 1.4 bitcast_convert_fusion.1
  323.5 1.0 convert_element_type.35
  324.6 0.6 fusion.2
  325.1 2.0 bitcast_convert_fusion
  327.2 0.6 fusion.1
  327.8 0.8 copy.48
  328.6 0.8 copy.49
  329.4 1.2 copy.50
  330.6 0.6 copy-done.5
  331.2 0.9 copy.51
  332.1 0.6 copy-done.4
  332.7 0.9 copy.52
  333.6 0.9 copy.53
  334.5 0.8 copy-done
  335.3 1.7 copy.54
  (28 shorter events, 0.1 us)
Async XLA Ops:
  315.6 5.4 %copy-start.11 = (bf16[224,1024]{1,0:T(8,128)(2,1)S(1)}, bf16[224,1024]{1,0:T(8,128)(2,1)}, u32[]{:S(2)}) copy-start(bf16[224,1024]{1,0:T(8,128)(2,1)} %get-tuple-element.69) | copy-start | bytes 1376260
  316.8 5.2 %copy-start.9 = (bf16[8,32,896]{2,1,0:T(8,128)(2,1)S(1)}, bf16[8,32,896]{2,1,0:T(8,128)(2,1)}, u32[]{:S(2)}) copy-start(bf16[8,32,896]{2,1,0:T(8,128)(2,1)} %get-tuple-element.75) | copy-start | bytes 1376260
  316.8 5.2 %copy-start.10 = (bf16[8,32,896]{2,1,0:T(8,128)(2,1)S(1)}, bf16[8,32,896]{2,1,0:T(8,128)(2,1)}, u32[]{:S(2)}) copy-start(bf16[8,32,896]{2,1,0:T(8,128)(2,1)} %get-tuple-element.70) | copy-start | bytes 1376260
  321.0 2.5 copy-start.8
  322.0 2.5 copy-start.12
  322.0 3.1 copy-start.2
  325.1 2.7 copy-start.6
  325.1 3.4 %copy-start.7 = (f32[128,896]{1,0:T(8,128)S(1)}, f32[128,896]{1,0:T(8,128)}, u32[]{:S(2)}) copy-start(f32[128,896]{1,0:T(8,128)} %get-tuple-element.65) | copy-start | bytes 1376260
  327.2 2.2 copy-start.1
  329.3 1.8 copy-start.5
  331.2 1.5 copy-start.4
  331.2 2.4 copy-start.3
  332.7 2.6 copy-start

commit v3 on v2

--- a/solution.py
+++ b/solution.py
@@ -555,8 +555,8 @@
             self.w,
         )
 
-    def start_z(self):
-        for j in (2, 3, 1):
+    def start_z(self, order=(2, 3, 1)):
+        for j in order:
             self.z_copy(j).start()
 
     def finish_z(self):
@@ -564,7 +564,14 @@
         for j in (1, 2, 3):
             self.z_copy(j).wait()
             total = total + self.part[j - 1].astype(f32)
-        self.share[...] = total.astype(bf16)
+        if len(self.share.shape) == 2:
+            self.share[...] = total.astype(bf16)
+            return
+        count = total.shape[0] // 4
+        blank = jnp.zeros((self.share.shape[1] - count, total.shape[1]), f32)
+        for place in range(4):
+            part = jnp.concatenate([total[place * count : (place + 1) * count], blank], axis=0)
+            self.share[place] = part.astype(bf16)
 
     def columns(self, place):
         width = self.spread
@@ -625,13 +632,10 @@
 
 def put_shares(target, grads, first=0):
     count = grads.shape[0] // 32
-    padded = target.shape[3]
-    for place in range(4):
-        for share in range(8):
-            start = (place * 8 + share) * count
-            part = grads[start : start + count]
-            part = jnp.concatenate([part, jnp.zeros((padded - count, part.shape[1]), f32)], axis=0)
-            target[share // 2, share % 2, place, :, first : first + part.shape[1]] = part.astype(bf16)
+    for share in range(8):
+        starts = [(place * 8 + share) * count for place in range(4)]
+        part = jnp.concatenate([grads[start : start + count] for start in starts], axis=0)
+        target[share // 2, share % 2, :, first : first + part.shape[1]] = part.astype(bf16)
 
 
 def put_rows(target, grads):
@@ -1211,8 +1215,6 @@
     down = CtxSum(send.take(12), recv.take(12), v.down_x, v.down_half, v.down_part, v.down_share)
     up = CtxSum(send.take(12), recv.take(12), v.up_x, v.up_half, v.up_part, v.up_share)
     cross = CtxSum(send.take(12), recv.take(12), v.cross_x, v.cross_half)
-    ctx_o = CtxSum(send.take(12), recv.take(12), v.cross_out_x, v.ctx_o_half)
-    out_o = CtxSum(send.take(12), recv.take(12), v.output_x, v.out_o_half)
     heads = SwapHeads(v.heads_grad, v.heads_out, False, send.take(8), recv.take(8))
     v.rows_o[0] = v.out_grad[...].astype(bf16)
 
@@ -1283,7 +1285,7 @@
     leaving.leave("pair_grad")
     normed_b = v.rows_b[...].reshape(rows, width)
     put_rows(v.cross_out_x, dot_tn(v.crossed[...], v.rows_two[...].reshape(rows, width)))
-    ctx_o.start_y()
+    leaving.leave("cross_out_x")
     put_shares(v.cross_x, dot_tn(normed_b, v.cross_grad[...]), 0)
     normed_grad = sum_b.total(v.keep[0])
     value = v.hidden_one[...]
@@ -1317,7 +1319,7 @@
     up.finish_y()
     up.start_z()
     cross.start_y()
-    out_o.start_y()
+    leaving.leave("output_x")
     leaving.leave("gains")
 
     per = tok // block
@@ -1333,9 +1335,6 @@
         if tile == 1:
             down.finish_z()
             leaving.leave("down_share")
-        if tile == 3:
-            ctx_o.finish_y()
-            leaving.leave("ctx_o_half")
 
     content_sum, position_sum = attend_back_tiles(
         v.qkv_order,
@@ -1364,8 +1363,6 @@
     leaving.leave("query_grad")
     cross.finish_y()
     leaving.leave("cross_half")
-    out_o.finish_y()
-    leaving.leave("out_o_half")
     up.finish_z()
     leaving.leave("up_share")
 
@@ -1395,9 +1392,9 @@
         table_grad=shape((seq_len, 128), f32),
         down_share=shape((hidden // 8, width), bf16),
         up_share=shape((4, padded, hidden), bf16),
-        cross_half=shape((4, 4, padded, 3 * cols), bf16),
-        ctx_o_half=shape((4, cols // 8, width), bf16),
-        out_o_half=shape((4, cols // 8, width), bf16),
+        cross_half=shape((4, width // 8, 3 * cols), bf16),
+        cross_out_x=shape((4, 2, cols // 8, width), bf16),
+        output_x=shape((4, 2, cols // 8, width), bf16),
     )
     results = {name + "_any": value for name, value in kept.items()}
     scratch = dict(
@@ -1413,8 +1410,6 @@
         dkey=vmem((seq_len, 128), f32),
         dvalue=vmem((seq_len, 128), f32),
         drel=vmem((seq_len + TILE, 128), f32),
-        cross_out_x=vmem((4, 2, cols // 8, width), bf16),
-        output_x=vmem((4, 2, cols // 8, width), bf16),
         count_far=vmem((7, 8, 128), f32),
         tokens_all=vmem((8, tok, width), bf16),
         pair=vmem((width, 512), bf16),
@@ -1452,10 +1447,10 @@
         down_x=vmem((4, 2, hidden // 8, width), bf16),
         down_half=vmem((4, hidden // 8, width), bf16),
         down_part=vmem((3, hidden // 8, width), bf16),
-        up_x=vmem((4, 2, 4, padded, hidden), bf16),
-        up_half=vmem((4, 4, padded, hidden), bf16),
-        up_part=vmem((3, 4, padded, hidden), bf16),
-        cross_x=vmem((4, 2, 4, padded, 3 * cols), bf16),
+        up_x=vmem((4, 2, width // 8, hidden), bf16),
+        up_half=vmem((4, width // 8, hidden), bf16),
+        up_part=vmem((3, width // 8, hidden), bf16),
+        cross_x=vmem((4, 2, width // 8, 3 * cols), bf16),
         send=dma((232,)),
         recv=dma((232,)),
         local=dma((24,)),
@@ -1583,7 +1578,7 @@
     c, w = places_here()
     send, recv, local = Pool(v.send), Pool(v.recv), Pool(v.local)
     tok, width = v.tokens.shape
-    cols = v.out_o_half.shape[1] * 8
+    cols = v.output_x.shape[2] * 8
     share = width // 4
 
     def load(source, target):
@@ -1606,8 +1601,8 @@
         for out in (v.down_out, v.up_all, v.cross_all, v.cross_o_out, v.output_out, v.pair_all)
     )
     cross_sum = summed(None, v.cross_half, v.cross_part, v.cross_share)
-    ctx_o_sum = summed(None, v.ctx_o_half, v.ctx_o_part, v.ctx_o_share)
-    out_o_sum = summed(None, v.out_o_half, v.out_o_part, v.out_o_share)
+    ctx_o_sum = summed(v.cross_out_x, v.ctx_o_half, v.ctx_o_part, v.ctx_o_share)
+    out_o_sum = summed(v.output_x, v.out_o_half, v.out_o_part, v.out_o_share)
     up_spread = Spread(v.up_share, v.up_all, send.take(4), recv.take(4))
     cross_spread = Spread(v.cross_share, v.cross_all, send.take(4), recv.take(4))
     sum_pair = SumRows(v.pair_give, v.pair_take, send.take(3), recv.take(3))
@@ -1646,11 +1641,11 @@
     ]
     v.down_out[c] = v.down_share[...]
     meet_lines()
+    down.start()
     up_spread.start()
-    cross_sum.start_z()
-    down.start()
-    ctx_o_sum.start_z()
-    out_o_sum.start_z()
+    cross_sum.start_z((2,))
+    ctx_o_sum.start_y()
+    out_o_sum.start_y()
     for copy in own_blocks:
         copy.start()
 
@@ -1660,18 +1655,23 @@
     for copy in loads:
         copy.wait()
     mixed = dot_tn(v.normed_a[...], query_grad)
+    up_spread.finish()
+    up.start()
+    down.step(0)
+    cross_sum.start_z((3, 1))
     turned = dot_tn(v.waves[...], high) + dot_tn(v.waves[...], low)
     for place in range(4):
         at = place * share
         v.sums[place] = jnp.concatenate([mixed[at : at + share], turned[at : at + share]], axis=1)
     sum_pair.give_far(v.sums[w ^ 3])
     sum_pair.give_near(v.sums[w ^ 1])
-    up_spread.finish()
-    up.start()
+    down.step(1)
+    up.step(0)
+    ctx_o_sum.finish_y()
+    ctx_o_sum.start_z()
+    out_o_sum.finish_y()
+    out_o_sum.start_z()
     sum_pair.pass_on(v.sums[w ^ 2])
-    down.step(0)
-    v.pair_all[c] = sum_pair.total(v.sums[w]).astype(bf16)
-    pair.start()
     for copy in late:
         copy.wait()
     near_count = v.near_grad.shape[0]
@@ -1681,12 +1681,14 @@
 
     sum_near.give_far(near_part(3))
     sum_near.give_near(near_part(1))
+    v.pair_all[c] = sum_pair.total(v.sums[w]).astype(bf16)
+    pair.start()
+    up.step(1)
+    down.step(2)
     cross_sum.finish_z()
     cross_spread.start()
     sum_near.pass_on(near_part(2))
     v.near_grad[...] = near_part(0)
-    up.step(0)
-    down.step(1)
     cross_spread.finish()
     cross.start()
     for j in (4, 6, 5, 7, 2, 3, 1):
@@ -1694,21 +1696,19 @@
             block_copy(j, m, c).start()
     for weight in weights:
         weight.start()
+    up.step(2)
+    pair.step(0)
     ctx_o_sum.finish_z()
     v.cross_o_out[c] = v.ctx_o_share[...]
     ctx_o.start()
     out_o_sum.finish_z()
     v.output_out[c] = v.out_o_share[...]
     out_o.start()
-    up.step(1)
     cross.step(0)
-    pair.step(0)
-    down.step(2)
+    pair.step(1)
     ctx_o.step(0)
     out_o.step(0)
-    up.step(2)
     cross.step(1)
-    pair.step(1)
     ctx_o.step(1)
     out_o.step(1)
 
@@ -1785,7 +1785,7 @@
     near = given["near_any"].shape[0]
     padded = given["up_share"].shape[1]
     hidden = given["up_share"].shape[2]
-    cols = given["out_o_half"].shape[1] * 8
+    cols = given["output_x"].shape[2] * 8
     share = width // 4
     any_space = pl.BlockSpec(memory_space=pl.ANY)
     shape = jax.ShapeDtypeStruct
@@ -1820,8 +1820,10 @@
         up_all=vmem((8, padded, 4 * hidden), bf16),
         cross_all=vmem((8, padded, 12 * cols), bf16),
         pair_all=vmem((8, share, 512), bf16),
-        cross_part=vmem((3, 4, padded, 3 * cols), bf16),
+        cross_part=vmem((3, width // 8, 3 * cols), bf16),
         cross_share=vmem((4, padded, 3 * cols), bf16),
+        ctx_o_half=vmem((4,) + part, bf16),
+        out_o_half=vmem((4,) + part, bf16),
         ctx_o_part=vmem((3,) + part, bf16),
         ctx_o_share=vmem(part, bf16),
         out_o_part=vmem((3,) + part, bf16),
@@ -2331,8 +2333,8 @@
             down_share=done.down_share,
             up_share=done.up_share,
             cross_half=done.cross_half,
-            ctx_o_half=done.ctx_o_half,
-            out_o_half=done.out_o_half,
+            cross_out_x=done.cross_out_x,
+            output_x=done.output_x,
             one_grad=done.one_grad,
             tokens=tokens[0],
             gains=done.gains,

time: 344 us -> 335 us (0.974)
  Pallas kernels: 308 us -> 299 us
    pallas_call x1, Pallas kernels: 182 us -> 176 us  [layer(): pl.pallas_call(functools.partial(layer_kernel, names, total_tokens, block...]
where the time goes in v3:
time: 335 us; the launch traced here: 329 us
  Pallas kernels  299 us (89%)
  local copies, waits for them, and re-layouts  15.9 us (5%)
  other arithmetic  12.7 us (4%)
    pallas_call x1, Pallas kernels, layer(): pl.pallas_call(functools.partial(layer_kernel, names, total_tokens, block...  176 us
    pallas_call x1, Pallas kernels, finish(): pl.pallas_call(functools.partial(finish_kernel, names), out_shape=list(re...  123 us
    unnamed x33, local copies, waits for them, and re-layouts  9.22 us

profile of v3, /device:TPU:0, one launch (start us, length us, event | category | flops | bytes accessed | tf_op | source)
XLA Modules:
  0.0 328.6 jit_solution(14231191987893156570)
XLA Ops:
  0.7 1.3 select_reduce_fusion.refs_0_
  1.9 3.4 %concatenate.12 = bf16[1184]{0:T(1024)(128)(2,1)S(1)} concatenate(bf16[224]{0:T(256)(128)(2,1)} %param.39, bf16[224]{0:T(256)(128)(2,1)} %param.40, bf16[224]{0:T(256)(128)(2,1)} %param.41, bf16[256]{0:T(256)(128)(2,1)} %param.31, bf16[256]{0:T(256)(128)(2,1)} %param.32), dimensions={0} | concatenate | bytes 4736 | tf_op jit(solution)/shard_map/concatenate | solution.py:2309
  5.4 0.6 broadcast_in_dim.30.refs_5_
  6.0 0.1 rev.7
  6.1 0.5 multiply_cosine_fusion
  6.6 0.1 rev.6
  6.7 0.2 multiply_sine_fusion.1
  6.9 1.0 maximum_maximum_fusion.refs_6_
  7.9 175.5 %layer.1 = (f32[128,896]{1,0:T(8,128)}, f32[8,1024]{1,0:T(8,128)}, f32[8,896]{1,0:T(8,128)}, bf16[1024,896]{1,0:T(8,128)(2,1)}, bf16[1024,896]{1,0:T(8,128)(2,1)...) custom-call(s32[16]{0:T(128)} %select_reduce_fusion.refs_0_, ...), custom_call_target="tpu_custom_call" | custom-call | tf_op jit(solution)/shard_map/layer/pallas_call | solution.py:1463
  183.4 123.3 %finish.1 = (f32[128,896]{1,0:T(8,128)}, f32[512,896]{1,0:T(8,128)}, f32[8,1024]{1,0:T(8,128)}, bf16[8,112,896]{2,1,0:T(8,128)(2,1)}, f32[224,3584]{1,0:T(8,128)...) custom-call(bf16[8,128,384]{2,1,0:T(8,128)(2,1)} %get-tuple-element., ...), custom_call_target="tpu_custom_call" | custom-call | tf_op jit(solution)/shard_map/finish/pallas_call | solution.py:1844
  306.8 1.2 slice.26
  308.0 2.1 convert_element_type.30
  310.2 2.0 convert_element_type.31
  312.2 0.0 copy-done.11
  312.2 1.0 convert_element_type.32
  313.2 1.4 bitcast_convert_fusion.1
  314.7 0.0 copy-done.8
  314.7 1.0 convert_element_type.35
  315.7 0.0 copy-done.12
  315.7 0.6 fusion.2
  316.3 2.0 bitcast_convert_fusion
  318.3 0.6 fusion.1
  319.0 0.8 copy.48
  319.8 0.8 copy.49
  320.5 1.2 copy.50
  321.8 0.6 copy-done.5
  322.4 0.9 copy.51
  323.3 0.6 copy-done.4
  323.9 0.9 copy.52
  324.8 0.9 copy.53
  325.7 0.8 copy-done
  326.5 1.7 copy.54
  (28 shorter events, 0.1 us)
Async XLA Ops:
  306.8 5.4 %copy-start.11 = (bf16[224,1024]{1,0:T(8,128)(2,1)S(1)}, bf16[224,1024]{1,0:T(8,128)(2,1)}, u32[]{:S(2)}) copy-start(bf16[224,1024]{1,0:T(8,128)(2,1)} %get-tuple-element.69) | copy-start | bytes 1376260
  308.0 5.2 %copy-start.9 = (bf16[8,32,896]{2,1,0:T(8,128)(2,1)S(1)}, bf16[8,32,896]{2,1,0:T(8,128)(2,1)}, u32[]{:S(2)}) copy-start(bf16[8,32,896]{2,1,0:T(8,128)(2,1)} %get-tuple-element.75) | copy-start | bytes 1376260
  308.0 5.2 %copy-start.10 = (bf16[8,32,896]{2,1,0:T(8,128)(2,1)S(1)}, bf16[8,32,896]{2,1,0:T(8,128)(2,1)}, u32[]{:S(2)}) copy-start(bf16[8,32,896]{2,1,0:T(8,128)(2,1)} %get-tuple-element.70) | copy-start | bytes 1376260
  312.2 2.5 copy-start.8
  313.2 2.5 copy-start.12
  313.2 3.1 copy-start.2
  316.3 2.7 copy-start.6
  316.3 3.4 %copy-start.7 = (f32[128,896]{1,0:T(8,128)S(1)}, f32[128,896]{1,0:T(8,128)}, u32[]{:S(2)}) copy-start(f32[128,896]{1,0:T(8,128)} %get-tuple-element.65) | copy-start | bytes 1376260
  318.3 2.2 copy-start.1
  320.5 1.8 copy-start.5
  322.4 1.5 copy-start.4
  322.4 2.4 copy-start.3
  323.9 2.6 copy-start

commit v4 on v3

--- a/solution.py
+++ b/solution.py
@@ -2307,7 +2307,16 @@
             teacher=teacher[0],
             mask=valid_mask,
             gain_row=jnp.concatenate(
-                [attention_gain, cross_gain, feedforward_gain, content_bias, position_bias]
+                [
+                    row.astype(f32)
+                    for row in (
+                        attention_gain,
+                        cross_gain,
+                        feedforward_gain,
+                        content_bias,
+                        position_bias,
+                    )
+                ]
             )[None],
             tables=tables,
             neighbours=neighbours.reshape(-1, width),

time: 335 us -> 335 us (level)
  no operation moved by 1% of the time
where the time goes in v4:
time: 335 us; the launch traced here: 329 us
  Pallas kernels  299 us (89%)
  local copies, waits for them, and re-layouts  15.9 us (5%)
  other arithmetic  12.7 us (4%)
    pallas_call x1, Pallas kernels, layer(): pl.pallas_call(functools.partial(layer_kernel, names, total_tokens, block...  175 us
    pallas_call x1, Pallas kernels, finish(): pl.pallas_call(functools.partial(finish_kernel, names), out_shape=list(re...  123 us
    unnamed x33, local copies, waits for them, and re-layouts  9.22 us

profile of v4, /device:TPU:0, one launch (start us, length us, event | category | flops | bytes accessed | tf_op | source)
XLA Modules:
  0.0 328.6 jit_solution(10257384679933362303)
XLA Ops:
  0.7 1.3 select_reduce_fusion.refs_0_
  1.9 3.4 %concatenate.13 = bf16[1184]{0:T(1024)(128)(2,1)S(1)} concatenate(bf16[224]{0:T(256)(128)(2,1)} %param.39, bf16[224]{0:T(256)(128)(2,1)} %param.40, bf16[224]{0:T(256)(128)(2,1)} %param.41, bf16[256]{0:T(256)(128)(2,1)} %param.31, bf16[256]{0:T(256)(128)(2,1)} %param.32), dimensions={0} | concatenate | bytes 4736 | tf_op jit(solution)/shard_map/concatenate | solution.py:2309
  5.4 0.6 reshape.74.refs_5_
  6.0 0.1 rev.7
  6.1 0.5 multiply_cosine_fusion
  6.6 0.1 rev.6
  6.7 0.2 multiply_sine_fusion.1
  6.9 1.0 maximum_maximum_fusion.refs_6_
  7.9 175.5 %layer.1 = (f32[128,896]{1,0:T(8,128)}, f32[8,1024]{1,0:T(8,128)}, f32[8,896]{1,0:T(8,128)}, bf16[1024,896]{1,0:T(8,128)(2,1)}, bf16[1024,896]{1,0:T(8,128)(2,1)...) custom-call(s32[16]{0:T(128)} %select_reduce_fusion.refs_0_, ...), custom_call_target="tpu_custom_call" | custom-call | tf_op jit(solution)/shard_map/layer/pallas_call | solution.py:1463
  183.4 123.4 %finish.1 = (f32[128,896]{1,0:T(8,128)}, f32[512,896]{1,0:T(8,128)}, f32[8,1024]{1,0:T(8,128)}, bf16[8,112,896]{2,1,0:T(8,128)(2,1)}, f32[224,3584]{1,0:T(8,128)...) custom-call(bf16[8,128,384]{2,1,0:T(8,128)(2,1)} %get-tuple-element., ...), custom_call_target="tpu_custom_call" | custom-call | tf_op jit(solution)/shard_map/finish/pallas_call | solution.py:1844
  306.8 1.2 slice.26
  308.0 2.1 convert_element_type.35
  310.2 2.0 convert_element_type.36
  312.2 0.0 copy-done.11
  312.2 1.0 convert_element_type.37
  313.2 1.4 bitcast_convert_fusion.1
  314.7 1.0 convert_element_type.40
  315.7 0.0 copy-done.12
  315.7 0.6 fusion.2
  316.3 2.0 bitcast_convert_fusion
  318.3 0.6 fusion.1
  319.0 0.8 copy.48
  319.8 0.0 copy-done.7
  319.8 0.8 copy.49
  320.5 1.2 copy.50
  321.8 0.6 copy-done.5
  322.4 0.9 copy.51
  323.3 0.6 copy-done.4
  323.9 0.9 copy.52
  324.8 0.9 copy.53
  325.7 0.8 copy-done
  326.5 1.7 copy.54
  (28 shorter events, 0.1 us)
Async XLA Ops:
  306.8 5.4 %copy-start.11 = (bf16[224,1024]{1,0:T(8,128)(2,1)S(1)}, bf16[224,1024]{1,0:T(8,128)(2,1)}, u32[]{:S(2)}) copy-start(bf16[224,1024]{1,0:T(8,128)(2,1)} %get-tuple-element.69) | copy-start | bytes 1376260
  308.0 5.2 %copy-start.9 = (bf16[8,32,896]{2,1,0:T(8,128)(2,1)S(1)}, bf16[8,32,896]{2,1,0:T(8,128)(2,1)}, u32[]{:S(2)}) copy-start(bf16[8,32,896]{2,1,0:T(8,128)(2,1)} %get-tuple-element.75) | copy-start | bytes 1376260
  308.0 5.2 %copy-start.10 = (bf16[8,32,896]{2,1,0:T(8,128)(2,1)S(1)}, bf16[8,32,896]{2,1,0:T(8,128)(2,1)}, u32[]{:S(2)}) copy-start(bf16[8,32,896]{2,1,0:T(8,128)(2,1)} %get-tuple-element.70) | copy-start | bytes 1376260
  312.2 2.5 copy-start.8
  313.2 2.5 copy-start.12
  313.2 3.1 copy-start.2
  316.3 2.7 copy-start.6
  316.3 3.4 %copy-start.7 = (f32[128,896]{1,0:T(8,128)S(1)}, f32[128,896]{1,0:T(8,128)}, u32[]{:S(2)}) copy-start(f32[128,896]{1,0:T(8,128)} %get-tuple-element.65) | copy-start | bytes 1376260
  318.3 2.2 copy-start.1
  320.5 1.8 copy-start.5
  322.4 1.5 copy-start.4
  322.4 2.4 copy-start.3
  323.9 2.6 copy-start
